TPU v7x, 128 devices: a whole 4x4x4 slice. The times are simulated.
128 devices in a mesh: gx: 8 (over z, core), gy: 16 (over y, x).
Axes of the slice: x: 4, y: 4, z: 4, core: 2. Of those that a mesh axis runs over, the one named last changes fastest.
Arguments:
- item_table: bfloat16 [1048576, 256], P(('gx', 'gy')), may hold values from -0.625 to 0.625
- bilinear: bfloat16 [256, 1024], replicated, may hold values from -0.375 to 0.375
- requests: int32 [128, 128, 64], P(('gx', 'gy')), may hold values from -1 to 8191, as said below
- history: int32 [32768, 50], P(('gx', 'gy')), may hold values from 0 to 8191, as said below
- lengths: int32 [32768], P(('gx', 'gy')), may hold values from 10 to 50
- init_logits: float32 [32768, 50, 4], P(('gx', 'gy')), may hold values from -6 to 6
- interest_grad: float32 [32768, 4, 256], P(('gx', 'gy')), may hold values from -6 to 6
Outputs:
- interests: bfloat16 [32768, 4, 256], P(('gx', 'gy'))
- table_grad: float32 [1048576, 256], P(('gx', 'gy'))
Inputs may be any that keep to these rules, and one draw needn't show every extreme that they name: requests[r, o, c] is a row of table shard o asked by device r in slot c, or -1 for an unused slot; the used slots of a list come first, hold distinct rows, and number at least one; a few shards have full lists (64 used slots) from every device. history[u, l] = o * 64 + c names a used slot c of list o of the device holding user u (users are laid out 256 a device).
All inputs are finite; a program needn't handle non-finite values.
Results may differ from a plain program's by a relative error of at most 0.015.
Values may be sent and summed in bfloat16 or wider, within the bound.
A program may use at most 192 MiB of HBM per device.

v0:
```python
import jax
import jax.numpy as jnp
from jax import lax
from jax.sharding import PartitionSpec as P

ITERS = 3


squash_eps = 1e-06


def route_interests(behavior_rows, bilinear, lengths, init_logits):
    users_here, hist_count, feature_width = behavior_rows.shape
    interest_count = init_logits.shape[2]
    remapped_values = jnp.dot(
        behavior_rows.reshape(users_here * hist_count, feature_width),
        bilinear,
        preferred_element_type=jnp.float32,
    )
    remapped_values = remapped_values.astype(jnp.bfloat16).reshape(
        users_here, hist_count, interest_count, feature_width
    )
    positions = lax.broadcasted_iota(jnp.int32, (users_here, hist_count), 1)
    live_mask = (positions < lengths[:, None]).astype(jnp.float32)
    logits = init_logits
    interest_capsule = None
    for turn_no in range(ITERS):
        exponent = jnp.exp(logits)
        coupling_weight = (
            exponent / jnp.sum(exponent, axis=2, keepdims=True) * live_mask[:, :, None]
        )
        weighted_total = jnp.einsum(
            "rmq,rmqs->rqs",
            coupling_weight.astype(jnp.bfloat16),
            remapped_values,
            preferred_element_type=jnp.float32,
        )
        norm_sq = jnp.sum(weighted_total * weighted_total, axis=2, keepdims=True)
        interest_capsule = weighted_total * jnp.sqrt(norm_sq + squash_eps) / (1.0 + norm_sq)
        if turn_no + 1 < ITERS:
            routing_agreement_score = jnp.einsum(
                "mazc,mzc->maz",
                remapped_values,
                interest_capsule.astype(jnp.bfloat16),
                preferred_element_type=jnp.float32,
            )
            logits = logits + routing_agreement_score
    return interest_capsule


def local(item_table, bilinear, requests, history, lengths, init_logits, interest_grad):
    asked_ids = requests[0]
    owner_count, slot_count = asked_ids.shape
    local_table_rows, feature_width = item_table.shape
    wanted = lax.all_to_all(asked_ids, ("gx", "gy"), split_axis=0, concat_axis=0, tiled=True)
    found = jnp.take(item_table, jnp.maximum(wanted, 0).reshape(-1), axis=0).reshape(
        owner_count, slot_count, feature_width
    )
    fetched = lax.all_to_all(found, ("gx", "gy"), split_axis=0, concat_axis=0, tiled=True)
    fetched = fetched.reshape(owner_count * slot_count, feature_width)
    slot_flat = history.reshape(-1)
    behavior_rows = jnp.take(fetched, slot_flat, axis=0).reshape(
        history.shape[0], history.shape[1], feature_width
    )
    interest_capsule, pullback = jax.vjp(
        lambda given: route_interests(given, bilinear, lengths, init_logits), behavior_rows
    )
    (row_grad,) = pullback(interest_grad)
    slot_grads = jax.ops.segment_sum(
        row_grad.reshape(-1, feature_width).astype(jnp.float32),
        slot_flat,
        num_segments=owner_count * slot_count,
    )
    returned = lax.all_to_all(
        slot_grads.reshape(owner_count, slot_count, feature_width).astype(jnp.bfloat16),
        ("gx", "gy"),
        split_axis=0,
        concat_axis=0,
        tiled=True,
    ).astype(jnp.float32)
    returned = returned.reshape(owner_count * slot_count, feature_width)
    targets = jnp.where(wanted >= 0, wanted, local_table_rows).reshape(-1)
    table_grad = jax.ops.segment_sum(returned, targets, num_segments=local_table_rows + 1)[
        :local_table_rows
    ]
    return (interest_capsule.astype(jnp.bfloat16), table_grad)


def solution(mesh):
    placed = (
        P(("gx", "gy"), None),
        P(),
        P(("gx", "gy"), None, None),
        P(("gx", "gy"), None),
        P(("gx", "gy")),
        P(("gx", "gy"), None, None),
        P(("gx", "gy"), None, None),
    )
    return jax.shard_map(
        local,
        mesh=mesh,
        in_specs=placed,
        out_specs=(P(("gx", "gy"), None, None), P(("gx", "gy"), None)),
        check_vma=False,
    )
```

profile of v0, /device:TPU:1, one launch (start us, length us, event | category | flops | bytes accessed | tf_op | source)
XLA Modules:
  0.0 727.1 jit_solution(13702007988125878649)
XLA Ops:
  1.6 20.9 %all_to_all.22 = s32[128,1,64]{2,1,0:T(1,128)S(1)} all-to-all(s32[128,1,64]{2,1,0:T(1,128)S(1)} %bitcast.187), channel_id=1, replica_groups=mesh['gx'=8,'gy'=16] {'gx','gy'}, dimensions={0} | all-to-all | bytes 65536 | tf_op jit(solution)/shard_map/all_to_all | solution.py:55
  24.8 33.9 %gather_fusion = bf16[8192,256]{1,0:T(8,128)(2,1)} fusion(bf16[8192,256]{1,0:T(8,128)(2,1)} %param.7, s32[8192]{0:T(1024)S(1)} %broadcast_clamp_fusion), kind=kCustom, calls=%fused_computation | custom fusion | bytes 8421376 | tf_op jit(solution)/shard_map/jit(_take)/gather | solution.py:56
  58.7 5.2 broadcast_select_fusion
  64.0 6.2 all-to-all-start.1
  71.4 7.6 %copy.88 = f32[256,4,50]{1,2,0:T(8,128)} copy(f32[256,4,50]{0,1,2:T(4,128)S(1)} %convert_bitcast_fusion) | data formatting | bytes 409600 | tf_op jit(solution)/shard_map/convert.10
  79.2 42.5 %all-to-all-done.1 = bf16[128,64,256]{2,1,0:T(8,128)(2,1)} async-done(((bf16[128,64,256]{2,1,0:T(8,128)(2,1)}), bf16[128,64,256]{2,1,0:T(8,128)(2,1)}, u32[]{:S(2)}, u32[]{:S(2)}) %all-to-all-start.1) | async-done | bytes 4194336 | tf_op jit(solution)/shard_map/all_to_all | solution.py:59
  121.7 32.3 %gather_fusion.1 = bf16[12800,256]{1,0:T(8,128)(2,1)} fusion(bf16[8192,256]{1,0:T(8,128)(2,1)} %bitcast.5, s32[13312]{0:T(1024)S(1)} %pad_clamp_fusion), kind=kCustom, calls=%fused_computation.1 | custom fusion | bytes 13158400 | tf_op jit(solution)/shard_map/jit(_take)/gather | solution.py:62
  154.0 15.6 %convolution_convert_fusion = bf16[12800,1024]{1,0:T(8,128)(2,1)} fusion(bf16[256,1024]{1,0:T(8,128)(2,1)S(1)} %copy-done, bf16[12800,256]{1,0:T(8,128)(2,1)} %gather_fusion.1, pred[12800]{0:T(1024)(128)(4,1)S(1)} %compare_and_fusion), kind=kOutput, calls=%fused_computation.19 | convolution fusion | flops 6727270400 | bytes 33305088 | tf_op jit(solution)/shard_map/jvp()/dot_general | solution.py:15
  169.6 43.0 %reshape.235 = bf16[256,50,4,256]{3,2,1,0:T(4,128)(2,1)} reshape(bf16[12800,1024]{1,0:T(8,128)(2,1)} %convolution_convert_fusion) | data formatting | bytes 52428800 | tf_op jit(solution)/shard_map/jvp()/reshape | solution.py:20
  212.6 13.6 %fusion.27 = f32[256,4,1,256]{3,2,1,0:T(1,128)S(1)} fusion(bf16[256,50,4,1]{1,3,2,0:T(2,128)(2,1)S(1)} %copy.89, bf16[256,50,4,256]{3,2,1,0:T(4,128)(2,1)} %reshape.235), kind=kOutput, calls=%fused_computation.38 | convolution fusion | flops 26214400 | bytes 27365376 | tf_op jit(solution)/shard_map/jvp(rmq,rmqs->rqs)/dot_general | solution.py:32
  227.5 1.7 fusion.64
  229.2 12.8 %fusion.25 = f32[256,4,1,50]{3,2,1,0:T(1,128)S(1)} fusion(bf16[256,50,4,256]{3,2,1,0:T(4,128)(2,1)} %reshape.235, bf16[256,4,256,1]{2,1,0,3:T(4,128)(2,1)S(1)} %bitcast.182), kind=kOutput, calls=%fused_computation.36 | convolution fusion | flops 26214400 | bytes 26943488 | tf_op jit(solution)/shard_map/jvp(mazc,mzc->maz)/dot_general | solution.py:41
  244.0 1.1 copy.94
  245.1 13.7 %fusion.23 = f32[256,4,1,256]{3,2,1,0:T(1,128)S(1)} fusion(bf16[256,50,4,1]{1,3,2,0:T(2,128)(2,1)} %copy.94, bf16[256,50,4,256]{3,2,1,0:T(4,128)(2,1)} %reshape.235), kind=kOutput, calls=%fused_computation.34 | convolution fusion | flops 26214400 | bytes 27365376 | tf_op jit(solution)/shard_map/jvp(rmq,rmqs->rqs)/dot_general | solution.py:32
  260.1 1.5 fusion.63
  261.6 13.8 %fusion.21 = f32[256,4,1,50]{3,2,1,0:T(1,128)} fusion(bf16[256,50,4,256]{3,2,1,0:T(4,128)(2,1)} %reshape.235, bf16[256,4,256,1]{2,1,0,3:T(4,128)(2,1)S(1)} %bitcast.183), kind=kOutput, calls=%fused_computation.32 | convolution fusion | flops 26214400 | bytes 26943488 | tf_op jit(solution)/shard_map/jvp(mazc,mzc->maz)/dot_general | solution.py:41
  275.4 1.9 copy.97
  277.2 1.1 fusion.65
  279.8 1.1 copy.98
  280.9 13.7 %fusion.19 = f32[256,4,1,256]{3,2,1,0:T(1,128)S(1)} fusion(bf16[256,50,4,1]{1,3,2,0:T(2,128)(2,1)} %copy.98, bf16[256,50,4,256]{3,2,1,0:T(4,128)(2,1)} %reshape.235), kind=kOutput, calls=%fused_computation.30 | convolution fusion | flops 26214400 | bytes 27365376 | tf_op jit(solution)/shard_map/jvp(rmq,rmqs->rqs)/dot_general | solution.py:32
  296.9 3.8 multiply_reduce_fusion
  301.7 1.0 copy.76
  303.5 2.9 add_add_fusion.2
  307.5 13.9 %fusion.17 = bf16[256,4,1,50]{3,2,1,0:T(2,128)(2,1)} fusion(bf16[256,50,4,256]{3,2,1,0:T(4,128)(2,1)} %reshape.235, f32[256,4,256,1]{2,1,0,3:T(4,128)S(1)} %bitcast.177), kind=kOutput, calls=%fused_computation.28 | convolution fusion | flops 26214400 | bytes 27365376 | tf_op jit(solution)/shard_map/transpose(jvp(rmq,rmqs->rqs))/dot_general | solution.py:32
  321.4 1.3 copy.101
  323.3 1.0 bitcast_multiply_fusion.14
  324.4 1.3 copy.102
  325.6 13.7 %fusion.15 = bf16[256,4,1,256]{3,2,1,0:T(2,128)(2,1)S(1)} fusion(bf16[256,4,50,1]{2,3,1,0:T(2,128)(2,1)} %copy.102, bf16[256,50,4,256]{3,2,1,0:T(4,128)(2,1)} %reshape.235), kind=kOutput, calls=%fused_computation.26 | convolution fusion | flops 26214400 | bytes 26841088 | tf_op jit(solution)/shard_map/transpose(jvp(mazc,mzc->maz))/dot_general | solution.py:41
  340.4 8.1 %fusion.41 = (f32[256,4]{1,0:T(8,128)}, f32[256,4]{1,0:T(8,128)}) fusion(f32[256,4,1,256]{3,2,1,0:T(1,128)S(1)} %fusion.23, f32[256,4]{1,0:T(8,128)S(1)} %copy-done.15, f32[256,4]{1,0:T(8,128)S(1)} %copy.72, bf16[256,4,1,256]{3,2,1,0:T(2,128)(2,1)S(1)} %fusion.15, f32[256,4]{1,0:T(8,128)S(1)} %get-tuple-element.23), kind=kLoop, calls=%fused_computation.60 | loop fusion | flops 2095104 | bytes 1593344 | tf_op jit(solution)/shard_map/transpose(jvp())/reduce_sum | solution.py:39
  349.4 1.0 copy.81
  351.9 2.4 add_add_fusion.1
  355.3 12.9 %fusion.13 = bf16[256,4,1,50]{3,2,1,0:T(2,128)(2,1)S(1)} fusion(bf16[256,50,4,256]{3,2,1,0:T(4,128)(2,1)} %reshape.235, f32[256,4,256,1]{2,1,0,3:T(4,128)S(1)} %bitcast.176), kind=kOutput, calls=%fused_computation.24 | convolution fusion | flops 26214400 | bytes 27365376 | tf_op jit(solution)/shard_map/transpose(jvp(rmq,rmqs->rqs))/dot_general | solution.py:32
  368.6 1.0 fusion.56
  371.0 13.7 %fusion.11 = bf16[256,4,1,256]{3,2,1,0:T(2,128)(2,1)S(1)} fusion(bf16[256,4,50,1]{2,3,1,0:T(2,128)(2,1)S(1)} %copy.106, bf16[256,50,4,256]{3,2,1,0:T(4,128)(2,1)} %reshape.235), kind=kOutput, calls=%fused_computation.22 | convolution fusion | flops 26214400 | bytes 26841088 | tf_op jit(solution)/shard_map/transpose(jvp(mazc,mzc->maz))/dot_general | solution.py:41
  384.7 8.2 %fusion.43 = (f32[256,4]{1,0:T(8,128)S(1)}, f32[256,4]{1,0:T(8,128)S(1)}) fusion(f32[256,4,1,256]{3,2,1,0:T(1,128)S(1)} %fusion.27, f32[256,4]{1,0:T(8,128)} %get-tuple-element.26, f32[256,4]{1,0:T(8,128)} %copy-done.8, bf16[256,4,1,256]{3,2,1,0:T(2,128)(2,1)S(1)} %fusion.11, f32[256,4]{1,0:T(8,128)} %copy-done.7), kind=kLoop, calls=%fused_computation.62 | loop fusion | flops 2095104 | bytes 1593344 | tf_op jit(solution)/shard_map/transpose(jvp())/reduce_sum | solution.py:39
  393.9 2.7 add_add_fusion
  396.6 8.4 %copy.78 = f32[256,4,50]{1,2,0:T(8,128)} copy(f32[256,4,50]{0,1,2:T(4,128)} %get-tuple-element.8) | data formatting | bytes 409600 | tf_op jit(solution)/shard_map/convert.8
  405.0 8.4 %copy.83 = f32[256,4,50]{1,2,0:T(8,128)} copy(f32[256,4,50]{0,1,2:T(4,128)} %get-tuple-element.12) | data formatting | bytes 409600 | tf_op jit(solution)/shard_map/convert.9
  413.4 7.7 %copy.84 = f32[256,4,50]{1,2,0:T(8,128)} copy(f32[256,4,50]{0,1,2:T(4,128)S(1)} %bitcast.181) | data formatting | bytes 409600 | tf_op jit(solution)/shard_map/transpose(jvp(mazc,mzc->maz))/transpose | solution.py:41
  421.1 7.7 %copy.79 = f32[256,4,50]{1,2,0:T(8,128)} copy(f32[256,4,50]{0,1,2:T(4,128)S(1)} %bitcast.179) | data formatting | bytes 409600 | tf_op jit(solution)/shard_map/transpose(jvp(mazc,mzc->maz))/transpose | solution.py:41
  428.8 77.1 %fusion.5 = bf16[256,50,4,256]{3,2,1,0:T(4,128)(2,1)} fusion(f32[256,4,50]{1,2,0:T(8,128)} %copy.88, f32[256,4,256]{2,1,0:T(4,128)S(1)} %copy-done.5, f32[256,4,256]{2,1,0:T(4,128)} %get-tuple-element.14, f32[256,4,50]{1,2,0:T(8,128)} %copy.84, f32[256,4,50]{1,2,0:T(8,128)} %copy.83, f32[256,4,256]{2,1,0:T(4,128)S(1)} %copy-done.4, ...), kind=kLoop, calls=%fused_computation.14 | loop fusion | flops 183500800 | bytes 32481280 | tf_op jit(solution)/shard_map/transpose(jvp(rmq,rmqs->rqs))/add_any | solution.py:32
  505.8 18.4 %copy.108 = bf16[1600,8,4,256]{3,1,2,0:T(8,128)(2,1)} copy(bf16[1600,8,4,256]{3,2,1,0:T(4,128)(2,1)} %bitcast.171) | data formatting | bytes 52428800
  524.2 14.8 %fusion.10 = f32[12800,256]{1,0:T(8,128)} fusion(bf16[12800,1024]{1,0:T(8,128)(2,1)} %bitcast.172, bf16[256,1024]{1,0:T(8,128)(2,1)S(1)} %copy-done), kind=kOutput, calls=%fused_computation.21 | convolution fusion | flops 6717440000 | bytes 39845888 | tf_op jit(solution)/shard_map/transpose(jvp())/dot_general | solution.py:15
  539.0 73.2 %scatter_custom_fusion = f32[8192,256]{1,0:T(8,128)} fusion(s32[12800]{0:T(1024)} %copy-done.17, f32[12800,256]{1,0:T(8,128)} %fusion.10, f32[]{:T(128)} %constant.21.clone.1), kind=kCustom, calls=%fused_computation.45 | custom fusion | flops 3276800 | bytes 8389120 | tf_op jit(solution)/shard_map/scatter-add | solution.py:69
  612.2 3.8 convert_element_type.128
  616.0 56.9 %all_to_all.23 = bf16[128,64,256]{2,1,0:T(8,128)(2,1)} all-to-all(bf16[128,64,256]{2,1,0:T(8,128)(2,1)S(1)} %bitcast.173), channel_id=1, replica_groups=mesh['gx'=8,'gy'=16] {'gx','gy'}, dimensions={0} | all-to-all | bytes 8388608 | tf_op jit(solution)/shard_map/all_to_all | solution.py:74
  672.9 46.6 %scatter_custom_fusion.1 = f32[8193,256]{1,0:T(8,128)} fusion(s32[8192]{0:T(1024)} %bitcast.189, bf16[8192,256]{1,0:T(8,128)(2,1)} %bitcast.174, f32[]{:T(128)} %constant.21.clone.1), kind=kCustom, calls=%fused_computation.40 | custom fusion | flops 4194304 | bytes 12584448 | tf_op jit(solution)/shard_map/scatter-add | solution.py:83
  719.5 7.3 %slice.8 = f32[8192,256]{1,0:T(8,128)} slice(f32[8193,256]{1,0:T(8,128)} %scatter_custom_fusion.1), slice={[0:8192], [0:256]} | slice | bytes 16777216 | tf_op jit(solution)/shard_map/slice | solution.py:83
  (102 shorter events, 23.3 us)
Async XLA Ops:
  0.6 153.4 %copy-start = (bf16[256,1024]{1,0:T(8,128)(2,1)S(1)}, bf16[256,1024]{1,0:T(8,128)(2,1)}, u32[]{:S(2)}) copy-start(bf16[256,1024]{1,0:T(8,128)(2,1)} %param.8) | copy-start | bytes 1572868
  24.8 45.4 %copy-start.19 = (s32[256,50]{0,1:T(8,128)S(1)}, s32[256,50]{0,1:T(8,128)}, u32[]{:S(2)}) copy-start(s32[256,50]{0,1:T(8,128)} %param.10) | copy-start | bytes 153604
  24.8 45.9 %copy-start.22 = (s32[256]{0:T(256)S(1)}, s32[256]{0:T(256)}, u32[]{:S(2)}) copy-start(s32[256]{0:T(256)} %param.11) | copy-start | bytes 3076
  24.8 45.9 %copy-start.18 = (f32[256,50,4]{0,2,1:T(4,128)S(1)}, f32[256,50,4]{0,2,1:T(4,128)}, u32[]{:S(2)}) copy-start(f32[256,50,4]{0,2,1:T(4,128)} %param.12) | copy-start | bytes 614404
  64.0 57.7 %all-to-all-start.1 = ((bf16[128,64,256]{2,1,0:T(8,128)(2,1)}), bf16[128,64,256]{2,1,0:T(8,128)(2,1)}, u32[]{:S(2)}, u32[]{:S(2)}) async-start(bf16[128,64,256]{2,1,0:T(8,128)(2,1)} %broadcast_select_fusion), calls=%async_computation.1 | async-start | bytes 8388608 | tf_op jit(solution)/shard_map/all_to_all | solution.py:59
  70.7 83.3 %copy-start.17 = (s32[12800]{0:T(1024)}, s32[12800]{0:T(1024)S(1)}, u32[]{:S(2)}) copy-start(s32[12800]{0:T(1024)S(1)} %reshape.232) | copy-start | bytes 153604
  226.6 2.5 copy-start.20
  227.3 16.6 %copy-start.7 = (f32[256,4]{1,0:T(8,128)}, f32[256,4]{1,0:T(8,128)S(1)}, u32[]{:S(2)}) copy-start(f32[256,4]{1,0:T(8,128)S(1)} %get-tuple-element.27) | copy-start | bytes 12292
  227.5 16.5 %copy-start.8 = (f32[256,4]{1,0:T(8,128)}, f32[256,4]{1,0:T(8,128)S(1)}, u32[]{:S(2)}) copy-start(f32[256,4]{1,0:T(8,128)S(1)} %copy.70) | copy-start | bytes 12292
  242.5 2.6 copy-start.12
  259.2 19.8 %copy-start.21 = (f32[256,4]{0,1:T(4,128)}, f32[256,4]{0,1:T(4,128)S(1)}, u32[]{:S(2)}) copy-start(f32[256,4]{0,1:T(4,128)S(1)} %copy.71) | copy-start | bytes 12292
  278.4 2.6 copy-start.14
  294.6 1.0 copy-start.1
  295.6 27.1 %copy-start.16 = (f32[256,50]{0,1:T(8,128)S(1)}, f32[256,50]{0,1:T(8,128)}, u32[]{:S(2)}) copy-start(f32[256,50]{0,1:T(8,128)} %multiply_divide_fusion.4) | copy-start | bytes 153604
  306.5 1.0 copy-start.6
  322.7 0.6 copy-start.11
  325.6 14.7 %copy-start.15 = (f32[256,4]{1,0:T(8,128)S(1)}, f32[256,4]{1,0:T(8,128)}, u32[]{:S(2)}) copy-start(f32[256,4]{1,0:T(8,128)} %get-tuple-element.22) | copy-start | bytes 12292
  339.4 1.0 copy-start.2
  339.4 30.2 %copy-start.13 = (f32[256,50]{0,1:T(8,128)S(1)}, f32[256,50]{0,1:T(8,128)}, u32[]{:S(2)}) copy-start(f32[256,50]{0,1:T(8,128)} %copy-done.12) | copy-start | bytes 153604
  354.3 1.0 copy-start.3
  369.8 0.7 copy-start.9
  371.0 42.3 %copy-start.10 = (f32[256,50,4]{0,2,1:T(4,128)S(1)}, f32[256,50,4]{0,2,1:T(4,128)}, u32[]{:S(2)}) copy-start(f32[256,50,4]{0,2,1:T(4,128)} %copy-done.9) | copy-start | bytes 614404
  396.6 32.2 %copy-start.4 = (f32[256,4,256]{2,1,0:T(4,128)S(1)}, f32[256,4,256]{2,1,0:T(4,128)}, u32[]{:S(2)}) copy-start(f32[256,4,256]{2,1,0:T(4,128)} %copy-done.3) | copy-start | bytes 3145732
  396.6 32.2 %copy-start.5 = (f32[256,4,256]{2,1,0:T(4,128)S(1)}, f32[256,4,256]{2,1,0:T(4,128)}, u32[]{:S(2)}) copy-start(f32[256,4,256]{2,1,0:T(4,128)} %add_add_fusion) | copy-start | bytes 3145732
where the time goes:
time: 732 us; the launch traced here: 727 us
  other arithmetic  250 us (34%)
  local copies, waits for them, and re-layouts  197 us (27%)
  matrix products  152 us (21%)
  blocking collectives  77.8 us (11%)
  waiting for transfers between devices  42.5 us (6%)
    add_any x1, other arithmetic, route_interests(): jnp.einsum('rmq,rmqs->rqs', coupling_weight.astype(jnp.bfloat16), remappe...  77.1 us
    scatter-add x1, other arithmetic, local(): jax.ops.segment_sum(row_grad.reshape(-1, feature_width).astype(jnp.float3...  73.2 us
    dot_general x5, matrix products, route_interests(): jnp.einsum('rmq,rmqs->rqs', coupling_weight.astype(jnp.bfloat16), remappe...  67.9 us
    all_to_all x1, blocking collectives, local(): lax.all_to_all(slot_grads.reshape(owner_count, slot_count, feature_width)...  56.9 us
    dot_general x4, matrix products, route_interests(): jnp.einsum('mazc,mzc->maz', remapped_values, interest_capsule.astype(jnp....  54 us
    scatter-add x1, other arithmetic, local(): jax.ops.segment_sum(returned, targets, num_segments=local_table_rows + 1)  46.6 us
    reshape x1, local copies, waits for them, and re-layouts, route_interests(): remapped_values.astype(jnp.bfloat16)  43 us
    all_to_all x1, waiting for transfers between devices, local(): lax.all_to_all(found, ('gx', 'gy'), split_axis=0, concat_axis=0, tiled=True)  42.5 us
  transfers between devices with their start and end apart: 1, of which 1 were waited for; matrix products, arithmetic and copies ran while one was open for 1% of the time, Pallas kernels for 0%

commit v1 on v0

v1 whole, which is shorter than its diff:
```python
import functools

import jax
import jax.numpy as jnp
from jax import lax
from jax.experimental import pallas as pl
from jax.experimental.pallas import tpu as pltpu
from jax.sharding import PartitionSpec as P

ITERS = 3
EPS = 1e-06
LP = 64
UG = 8
HALF = 128
MIB = 1024 * 1024
F32 = jnp.float32
BF16 = jnp.bfloat16


def vmem():
    return pl.BlockSpec(memory_space=pltpu.VMEM)


def smem():
    return pl.BlockSpec(memory_space=pltpu.SMEM)


def two(i):
    return pl.ds(pl.multiple_of(2 * i, 2), 2)


def split_rows(src, dst, rows, step=512):
    def body(c, carry):
        at = pl.multiple_of(c * step, step)
        for h in range(2):
            dst[pl.ds(2 * at + h, step, stride=2), :] = src[
                pl.ds(at, step), h * HALF : (h + 1) * HALF
            ].astype(F32)
        return carry

    lax.fori_loop(0, rows // step, body, 0)


def fetch_kernel(slots, ids, table, out, wide, stage):
    rows = table.shape[0]
    split_rows(table, wide, rows)

    def body(c, carry):
        for j in range(slots):
            stage[pl.ds(2 * j, 2), :] = wide[two(ids[c * slots + j]), :]
        out[pl.ds(pl.multiple_of(c * 2 * slots, 2 * slots), 2 * slots), :] = stage[...].astype(BF16)
        return carry

    lax.fori_loop(0, ids.shape[0] // slots, body, 0)


def fetch_rows(ids, table, slots):
    rows = table.shape[0]
    return pl.pallas_call(
        functools.partial(fetch_kernel, slots),
        name="fetch_rows",
        out_shape=jax.ShapeDtypeStruct((2 * ids.shape[0], HALF), BF16),
        in_specs=[smem(), vmem()],
        out_specs=vmem(),
        scratch_shapes=[pltpu.VMEM((2 * rows, HALF), F32), pltpu.VMEM((2 * slots, HALF), F32)],
        compiler_params=pltpu.CompilerParams(vmem_limit_bytes=40 * MIB),
    )(ids, table)


def return_kernel(slots, ids, grads, out, total, stage):
    step = pl.program_id(0)
    feed = ids.shape[0] * 2 // grads.shape[0]
    chunk = grads.shape[0]

    @pl.when(step == 0)
    def _():
        def clear(c, carry):
            total[pl.ds(pl.multiple_of(c * 512, 512), 512), :] = jnp.zeros((512, HALF), F32)
            return carry

        lax.fori_loop(0, (total.shape[0] - 16) // 512, clear, 0)

    @pl.when(step < feed)
    def _():
        stage[...] = grads[...].astype(F32)

        def body(c, carry):
            for b in range(2):
                base = c * 64 + b * 32
                at = [two(ids[step * (chunk // 2) + base + j]) for j in range(32)]
                held = [total[at[j], :] for j in range(32)]
                for j in range(32):
                    total[at[j], :] = held[j] + stage[two(base + j), :]
            return carry

        lax.fori_loop(0, chunk // 128, body, 0)

    @pl.when(step >= feed)
    def _():
        rows = out.shape[0]
        at = pl.multiple_of((step - feed) * 2 * rows, 2 * rows)
        for h in range(2):
            out[:, h * HALF : (h + 1) * HALF] = total[pl.ds(at + h, rows, stride=2), :]


def return_rows(ids, grads, rows, slots):
    feed = 8
    drain = 8
    chunk = grads.shape[0] // feed
    return pl.pallas_call(
        functools.partial(return_kernel, slots),
        name="return_rows",
        grid=(feed + drain,),
        out_shape=jax.ShapeDtypeStruct((rows, 2 * HALF), F32),
        in_specs=[smem(), pl.BlockSpec((chunk, HALF), lambda i: (jnp.minimum(i, feed - 1), 0))],
        out_specs=pl.BlockSpec((rows // drain, 2 * HALF), lambda i: (jnp.maximum(i - feed, 0), 0)),
        scratch_shapes=[pltpu.VMEM((2 * rows + 16, HALF), F32), pltpu.VMEM((chunk, HALF), F32)],
        compiler_params=pltpu.CompilerParams(vmem_limit_bytes=40 * MIB),
    )(ids, grads)


def route_kernel(
    interests, hist_len,
    slots, fetched, bilinear, first_logits, live, cotangent, same,
    capsules, slot_grads,
    wide, rows, stage, logits, w0, w1, w2, z0, z1, pooled, q0, q1, g0, g1, g2, s0, s1, s2,
    same_buf, same_sem,
):
    groups = live.shape[0]
    width = UG * LP
    lines = interests * UG
    feature = rows.shape[1]

    def nt(a, b):
        return lax.dot_general(a, b, (((1,), (1,)), ((), ())), preferred_element_type=F32)

    def tn(a, b):
        return lax.dot_general(a, b, (((0,), (0,)), ((), ())), preferred_element_type=F32)

    def block(g):
        return rows[pl.ds(pl.multiple_of(g * width, width), width), :]

    def lanes(ref, g):
        return ref.at[pl.ds(pl.multiple_of(g * lines, lines), lines), :]

    def users(g):
        return pl.ds(pl.multiple_of(g * UG, UG), UG)

    def by_interest(value):
        return [value[k * UG : (k + 1) * UG] for k in range(interests)]

    def gathered(ref, g):
        return jnp.concatenate([ref[k, users(g), :] for k in range(interests)], axis=0).astype(BF16)

    def put_pooled(g, value):
        for k, part in enumerate(by_interest(value)):
            pooled[k, users(g), :] = part

    def mask_of(g):
        owner = lax.broadcasted_iota(jnp.int32, (UG, width), 0)
        lane = lax.broadcasted_iota(jnp.int32, (UG, width), 1)
        alive = jnp.broadcast_to(live[pl.ds(g, 1), :], (UG, width))
        return (lane // LP == owner) & (alive > 0.0)

    def coupling(value, g):
        powers = [jnp.exp(part) for part in by_interest(value)]
        scale = 1.0 / functools.reduce(jnp.add, powers)
        mask = mask_of(g)
        return jnp.concatenate([jnp.where(mask, p * scale, 0.0) for p in powers], axis=0)

    def coupling_grad(weights, dots):
        ws, ds = by_interest(weights), by_interest(dots)
        inner = functools.reduce(jnp.add, [w * d for w, d in zip(ws, ds)])
        return jnp.concatenate([w * (d - inner) for w, d in zip(ws, ds)], axis=0)

    def loop(count, body):
        lax.fori_loop(0, count, lambda i, c: (body(i), c)[1], 0)

    def over_groups(stages, unroll=2):
        def body(i):
            ids = [i * unroll + j for j in range(unroll)]
            held = [() for _ in ids]
            for stage_fn in stages:
                held = [stage_fn(g, *h) for g, h in zip(ids, held)]

        loop(groups // unroll, body)

    def mapping(k):
        return bilinear[:, k * feature : (k + 1) * feature]

    def squash(summed):
        size = jnp.sum(summed * summed, axis=1, keepdims=True)
        root = jnp.sqrt(size + EPS)
        return size, root, root / (1.0 + size)

    def forward(keep, out):
        for k in range(interests):
            summed = jnp.dot(pooled[k].astype(BF16), mapping(k), preferred_element_type=F32)
            keep[k] = summed
            _, _, factor = squash(summed)
            out[k] = nt((summed * factor).astype(BF16), mapping(k))

    def squash_grad(summed, given):
        size, root, factor = squash(summed)
        along = jnp.sum(summed * given, axis=1, keepdims=True)
        above = 1.0 + size
        slope = 1.0 / (root * above) - 2.0 * root / (above * above)
        return given * factor + summed * (slope * along), factor

    def backward(keep, out):
        for k in range(interests):
            given = jnp.dot(pooled[k].astype(BF16), mapping(k), preferred_element_type=F32)
            grad, _ = squash_grad(keep[k], given)
            out[k] = nt(grad.astype(BF16), mapping(k))

    split_dense = 1024

    def widen(c):
        at = pl.ds(pl.multiple_of(c * split_dense, split_dense), split_dense)
        wide[at, :] = fetched[at, :].astype(F32)

    loop(fetched.shape[0] // split_dense, widen)
    stage[...] = jnp.zeros_like(stage)

    def first(g):
        for u in range(UG):
            for l in range(hist_len):
                slot = slots[g * (UG * hist_len) + u * hist_len + l]
                stage[pl.ds(2 * (u * LP + l), 2), :] = wide[two(slot), :]
        at = pl.ds(pl.multiple_of(g * width, width), width)
        for h in range(2):
            rows[at, h * HALF : (h + 1) * HALF] = stage[pl.ds(h, width, stride=2), :].astype(BF16)
        start = jnp.concatenate(
            [
                jnp.broadcast_to(first_logits[pl.ds(g * interests + k, 1), :], (UG, width))
                for k in range(interests)
            ],
            axis=0,
        )
        lanes(logits, g)[...] = start
        weights = coupling(start, g)
        lanes(w0, g)[...] = weights
        put_pooled(g, jnp.dot(weights.astype(BF16), block(g), preferred_element_type=F32))

    loop(groups, first)
    forward(s0, q0)

    def turn(q, w, last):
        def agree(g):
            return (nt(gathered(q, g), block(g)),)

        def reweigh(g, scores):
            value = lanes(logits, g)[...] + scores
            if not last:
                lanes(logits, g)[...] = value
            weights = coupling(value, g)
            lanes(w, g)[...] = weights
            return (weights.astype(BF16),)

        def pool(g, weights):
            put_pooled(g, jnp.dot(weights, block(g), preferred_element_type=F32))
            return ()

        over_groups([agree, reweigh, pool])

    turn(q0, w1, False)
    forward(s1, q1)
    turn(q1, w2, True)

    for k in range(interests):
        summed = jnp.dot(pooled[k].astype(BF16), mapping(k), preferred_element_type=F32)
        grad, factor = squash_grad(summed, cotangent[k])
        capsules[k] = (summed * factor).astype(BF16)
        g2[k] = nt(grad.astype(BF16), mapping(k))

    def turn_back(gr, w, z, add):
        def dots(g):
            return (nt(gathered(gr, g), block(g)),)

        def reweigh(g, value):
            grad = coupling_grad(lanes(w, g)[...], value)
            if add:
                grad = grad + lanes(logits, g)[...]
            else:
                lanes(logits, g)[...] = grad
            grad = grad.astype(BF16)
            lanes(z, g)[...] = grad
            return (grad,)

        def pool(g, grad):
            put_pooled(g, jnp.dot(grad, block(g), preferred_element_type=F32))
            return ()

        over_groups([dots, reweigh, pool])

    turn_back(g2, w2, z1, False)
    backward(s1, g1)
    turn_back(g1, w1, z0, True)
    backward(s0, g0)

    def copy_same(g):
        slot = lax.rem(g, 2)
        return pltpu.make_async_copy(
            same.at[pl.ds(pl.multiple_of(g * width, width), width), :],
            same_buf.at[slot],
            same_sem.at[slot],
        )

    copy_same(0).start()

    def clear(c):
        at = pl.ds(pl.multiple_of(c * split_dense, split_dense), split_dense)
        wide[at, :] = jnp.zeros((split_dense, HALF), F32)

    loop(fetched.shape[0] // split_dense, clear)

    def last(g):
        coefs = jnp.concatenate(
            [lanes(w, g)[...].astype(BF16) for w in (w0, w1, w2)]
            + [lanes(z, g)[...] for z in (z0, z1)],
            axis=0,
        )
        basis = jnp.concatenate([gathered(b, g) for b in (g0, g1, g2, q0, q1)], axis=0)
        grads = tn(coefs, basis).astype(BF16)

        @pl.when(g + 1 < groups)
        def _():
            copy_same(g + 1).start()

        copy_same(g).wait()
        part = width // 2
        for p in range(2):
            merged = jnp.dot(
                same_buf[lax.rem(g, 2), p * part : (p + 1) * part, :],
                grads[p * part : (p + 1) * part],
                preferred_element_type=F32,
            )
            for h in range(2):
                stage[pl.ds(2 * p * part + h, part, stride=2), :] = merged[:, h * HALF : (h + 1) * HALF]
        batch = hist_len // 2
        for u in range(UG):
            for b in range(2):
                ls = range(b * batch, (b + 1) * batch)
                at = [two(slots[g * (UG * hist_len) + u * hist_len + l]) for l in ls]
                held = [wide[a, :] for a in at]
                for a, value, l in zip(at, held, ls):
                    wide[a, :] = value + stage[pl.ds(2 * (u * LP + l), 2), :]

    loop(groups, last)

    def emit(c):
        at = pl.ds(pl.multiple_of(c * split_dense, split_dense), split_dense)
        slot_grads[at, :] = wide[at, :].astype(BF16)

    loop(fetched.shape[0] // split_dense, emit)


def route(slots, fetched, bilinear, lengths, init_logits, interest_grad):
    users_here, hist_len, interests = init_logits.shape
    feature = bilinear.shape[0]
    groups = users_here // UG
    width = UG * LP
    pad = LP - hist_len
    ids = jnp.pad(slots, ((0, 0), (0, pad)), constant_values=-1).reshape(users_here // 4, 4 * LP)
    place = jnp.arange(4 * LP, dtype=jnp.int32)
    batch = place // LP * 2 + (place % LP >= hist_len // 2)
    same = (ids[:, :, None] == ids[:, None, :]) & (batch[:, None] == batch[None, :])
    same = same.astype(BF16).reshape(users_here * LP, 4 * LP)
    live = (jnp.arange(LP, dtype=jnp.int32)[None, :] < lengths[:, None]).astype(F32)
    live = live.reshape(groups, width)
    first_logits = jnp.pad(jnp.transpose(init_logits, (0, 2, 1)), ((0, 0), (0, 0), (0, pad)))
    first_logits = first_logits.reshape(groups, UG, interests, LP)
    first_logits = jnp.transpose(first_logits, (0, 2, 1, 3)).reshape(groups * interests, width)
    cotangent = jnp.transpose(interest_grad, (1, 0, 2))
    lines = groups * interests * UG
    per_user = pltpu.VMEM((interests, users_here, feature), F32)
    capsules, slot_grads = pl.pallas_call(
        functools.partial(route_kernel, interests, hist_len),
        name="route_users",
        out_shape=(
            jax.ShapeDtypeStruct((interests, users_here, feature), BF16),
            jax.ShapeDtypeStruct(fetched.shape, BF16),
        ),
        in_specs=[smem()] + [vmem()] * 5 + [pl.BlockSpec(memory_space=pl.ANY)],
        out_specs=(vmem(), vmem()),
        scratch_shapes=[
            pltpu.VMEM(fetched.shape, F32),
            pltpu.VMEM((users_here * LP, feature), BF16),
            pltpu.VMEM((2 * width, HALF), F32),
        ]
        + [pltpu.VMEM((lines, width), F32)] * 4
        + [pltpu.VMEM((lines, width), BF16)] * 2
        + [per_user] * 9
        + [pltpu.VMEM((2, width, 4 * LP), BF16), pltpu.SemaphoreType.DMA((2,))],
        compiler_params=pltpu.CompilerParams(vmem_limit_bytes=60 * MIB),
    )(slots.reshape(-1), fetched, bilinear, first_logits, live, cotangent, same)
    return jnp.transpose(capsules, (1, 0, 2)), slot_grads


def local(item_table, bilinear, requests, history, lengths, init_logits, interest_grad):
    asked = requests[0]
    owners, slots = asked.shape
    table_rows = item_table.shape[0]

    def exchange(value):
        return lax.all_to_all(value, ("gx", "gy"), split_axis=0, concat_axis=0, tiled=True)

    wanted = exchange(asked).reshape(-1)
    found = fetch_rows(jnp.maximum(wanted, 0), item_table, slots)
    fetched = exchange(found)
    capsules, slot_grads = route(history, fetched, bilinear, lengths, init_logits, interest_grad)
    returned = exchange(slot_grads)
    targets = jnp.where(wanted >= 0, wanted, table_rows)
    return capsules, return_rows(targets, returned, table_rows, slots)


def solution(mesh):
    both = ("gx", "gy")
    placed = (
        P(both, None),
        P(),
        P(both, None, None),
        P(both, None),
        P(both),
        P(both, None, None),
        P(both, None, None),
    )
    return jax.shard_map(
        local,
        mesh=mesh,
        in_specs=placed,
        out_specs=(P(both, None, None), P(both, None)),
        check_vma=False,
    )
```

time: 732 us -> 272 us (0.37)
  other arithmetic: 250 us -> 7.46 us
  local copies, waits for them, and re-layouts: 197 us -> 10.7 us
  matrix products: 152 us -> 0 us
  Pallas kernels: 0 us -> 129 us
  blocking collectives: 77.8 us -> 20.9 us
  waiting for transfers between devices: 42.5 us -> 91.3 us
    dot_general x11 -> x0, matrix products: 152 us -> none  [the longest x5 67.9 us: route_interests(): jnp.einsum('rmq,rmqs->rqs', coupling_weight.astype(jnp.bfloat16), remappe...]
    pallas_call x0 -> x3, Pallas kernels: none -> 129 us  [the longest x1 93.5 us: route(): pl.pallas_call(functools.partial(route_kernel, interests, hist_len), name...]
    scatter-add x2 -> x0, other arithmetic: 120 us -> none  [the longest x1 73.2 us: local(): jax.ops.segment_sum(row_grad.reshape(-1, feature_width).astype(jnp.float3...]
    add_any x8 -> x0, other arithmetic: 86.6 us -> none  [the longest x1 77.1 us: route_interests(): jnp.einsum('rmq,rmqs->rqs', coupling_weight.astype(jnp.bfloat16), remappe...]
    gather x2 -> x0, local copies, waits for them, and re-layouts: 66.3 us -> none  [the longest x1 33.9 us: local(): jnp.take(item_table, jnp.maximum(wanted, 0).reshape(-1), axis=0)]
    all_to_all x2 -> x1, blocking collectives: 77.8 us -> 20.9 us  [exchange(): lax.all_to_all(value, ('gx', 'gy'), split_axis=0, concat_axis=0, tiled=True)]
    all_to_all x1 -> x2, waiting for transfers between devices: 42.5 us -> 91.3 us  [exchange(): lax.all_to_all(value, ('gx', 'gy'), split_axis=0, concat_axis=0, tiled=True)]
    reshape x3, local copies, waits for them, and re-layouts: 43.3 us -> 1.7 us  [the longest x1 0.87 us: route(): jnp.transpose(first_logits, (0, 2, 1, 3)).reshape(groups * interests, width)]
  transfers between devices with their start and end apart: 1 -> 2, of which waited for: 1 -> 2; matrix products, arithmetic and copies ran while one was open for 1% -> 4% of each run, Pallas kernels for 0% -> 0%
where the time goes in v1:
time: 272 us; the launch traced here: 271 us
  Pallas kernels  129 us (47%)
  waiting for transfers between devices  91.3 us (34%)
  blocking collectives  20.9 us (8%)
  starting transfers between devices  11.3 us (4%)
  local copies, waits for them, and re-layouts  10.7 us (4%)
  other arithmetic  7.46 us (3%)
    pallas_call x1, Pallas kernels, route(): pl.pallas_call(functools.partial(route_kernel, interests, hist_len), name...  93.5 us
    all_to_all x2, waiting for transfers between devices, exchange(): lax.all_to_all(value, ('gx', 'gy'), split_axis=0, concat_axis=0, tiled=True)  91.3 us
    pallas_call x1, Pallas kernels, return_rows(): pl.pallas_call(functools.partial(return_kernel, slots), name='return_rows...  22.4 us
    all_to_all x1, blocking collectives, exchange(): lax.all_to_all(value, ('gx', 'gy'), split_axis=0, concat_axis=0, tiled=True)  20.9 us
    pallas_call x1, Pallas kernels, fetch_rows(): pl.pallas_call(functools.partial(fetch_kernel, slots), name='fetch_rows',...  12.7 us
    all_to_all x2, starting transfers between devices, exchange(): lax.all_to_all(value, ('gx', 'gy'), split_axis=0, concat_axis=0, tiled=True)  11.3 us
    unnamed x19, local copies, waits for them, and re-layouts  7.81 us
    convert_element_type x1, other arithmetic, route(): same = same.astype(BF16).reshape(users_here * LP, 4 * LP)  5.9 us
  transfers between devices with their start and end apart: 2, of which 2 were waited for; matrix products, arithmetic and copies ran while one was open for 4% of the time, Pallas kernels for 0%

profile of v1, /device:TPU:1, one launch (start us, length us, event | category | flops | bytes accessed | tf_op | source)
XLA Modules:
  0.0 271.1 jit_solution(7584755765499860234)
XLA Ops:
  0.6 0.8 copy.21
  1.5 20.9 %all_to_all.31 = s32[128,1,64]{2,1,0:T(1,128)S(1)} all-to-all(s32[128,1,64]{2,1,0:T(1,128)S(1)} %bitcast.29), channel_id=1, replica_groups=mesh['gx'=8,'gy'=16] {'gx','gy'}, dimensions={0} | all-to-all | bytes 65536 | tf_op jit(solution)/shard_map/all_to_all | solution.py:406
  22.4 0.5 broadcast.146
  22.9 0.8 reduce.3
  23.7 0.1 reshape.113
  23.8 0.0 copy-start.1
  23.8 2.2 copy-done.1
  26.0 12.7 %fetch_rows.1 = bf16[16384,128]{1,0:T(8,128)(2,1)S(1)} custom-call(s32[8192]{0:T(1024)S(1)} %get-tuple-element.13.ids, bf16[8192,256]{1,0:T(8,128)(2,1)S(1)} %copy-done.1), custom_call_target="tpu_custom_call" | custom-call | tf_op jit(solution)/shard_map/fetch_rows/pallas_call | solution.py:59
  38.7 0.0 copy-start
  38.7 2.0 copy-done
  40.7 0.0 copy-start.5
  40.7 0.0 copy-start.6
  40.7 0.0 copy-start.4
  40.7 5.7 %all-to-all-start.1 = ((bf16[128,128,128]{2,1,0:T(8,128)(2,1)}), bf16[128,128,128]{2,1,0:T(8,128)(2,1)}, u32[]{:S(2)}, u32[]{:S(2)}) async-start(bf16[128,128,128]{2,1,0:T(8,128)(2,1)} %bitcast.24), calls=%async_computation.1 | async-start | bytes 8388608 | tf_op jit(solution)/shard_map/all_to_all | solution.py:406
  46.4 0.0 copy-done.5
  46.4 0.0 copy-start.2
  46.4 0.1 copy.20
  46.5 0.8 reshape.112.slots
  47.3 0.1 eq.41
  47.4 0.1 eq.39
  47.5 0.1 lt.29
  47.5 0.0 copy-done.6
  47.5 0.1 lt.31
  47.6 0.1 lt.32
  47.7 0.1 lt.33
  47.8 0.0 copy-done.4
  47.8 0.2 copy.22
  48.1 0.1 copy.23
  48.2 0.9 reshape.115.first_logits
  49.1 0.0 copy-done.2
  49.1 1.3 copy.30
  50.3 0.1 broadcast_compare_fusion
  50.4 5.9 %fusion.1.same = bf16[16384,256]{1,0:T(8,128)(2,1)} fusion(s32[64,256]{1,0:T(8,128)S(1)} %eq.41, s32[16384]{0:T(1024)S(1)} %eq.39, pred[256,256]{1,0:T(8,128)(4,1)S(1)} %broadcast_compare_fusion), kind=kLoop, calls=%fused_computation.2 | loop fusion | flops 12582912 | bytes 8585216 | tf_op jit(solution)/shard_map/convert_element_type | solution.py:368
  56.3 0.6 compare_convert_fusion.live
  57.0 41.0 %all-to-all-done.1 = bf16[128,128,128]{2,1,0:T(8,128)(2,1)} async-done(((bf16[128,128,128]{2,1,0:T(8,128)(2,1)}), bf16[128,128,128]{2,1,0:T(8,128)(2,1)}, u32[]{:S(2)}, u32[]{:S(2)}) %all-to-all-start.1) | async-done | bytes 4194336 | tf_op jit(solution)/shard_map/all_to_all | solution.py:406
  98.0 93.5 %route_users.1 = (bf16[4,256,256]{2,1,0:T(8,128)(2,1)}, bf16[16384,128]{1,0:T(8,128)(2,1)}) custom-call(s32[12800]{0:T(1024)} %reshape.112.slots, bf16[16384,128]{1,0:T(8,128)(2,1)} %bitcast.2.fetched, bf16[256,1024]{1,0:T(8,128)(2,1)} %bilinear.1, f32[128,512]{1,0:T(8,128)} %reshape.115.first_logits, f32[32,512]{1,0:T(8,128)} %compare_convert_fusion.live, ...), custom_call_target="tpu_custom_call" | custom-call | tf_op jit(solution)/shard_map/route_users/pallas_call | solution.py:377
  191.5 0.0 copy-start.3
  191.5 5.6 %all-to-all-start.2 = ((bf16[128,128,128]{2,1,0:T(8,128)(2,1)}), bf16[128,128,128]{2,1,0:T(8,128)(2,1)}, u32[]{:S(2)}, u32[]{:S(2)}) async-start(bf16[128,128,128]{2,1,0:T(8,128)(2,1)} %bitcast.26), calls=%async_computation.2 | async-start | bytes 8388608 | tf_op jit(solution)/shard_map/all_to_all | solution.py:406
  197.2 0.0 copy-done.3
  197.2 1.2 copy.27
  198.4 50.3 %all-to-all-done.2 = bf16[128,128,128]{2,1,0:T(8,128)(2,1)} async-done(((bf16[128,128,128]{2,1,0:T(8,128)(2,1)}), bf16[128,128,128]{2,1,0:T(8,128)(2,1)}, u32[]{:S(2)}, u32[]{:S(2)}) %all-to-all-start.2) | async-done | bytes 4194336 | tf_op jit(solution)/shard_map/all_to_all | solution.py:406
  248.7 22.4 %return_rows.1 = f32[8192,256]{1,0:T(8,128)} custom-call(s32[8192]{0:T(1024)S(1)} %get-tuple-element.12.ids, bf16[16384,128]{1,0:T(8,128)(2,1)} %bitcast.11.grads), custom_call_target="tpu_custom_call" | custom-call | tf_op jit(solution)/shard_map/return_rows/pallas_call | solution.py:110
  (5 shorter events, 0.1 us)
Async XLA Ops:
  23.8 2.2 copy-start.1
  38.7 2.0 copy-start
  40.7 5.7 %copy-start.5 = (s32[256,50]{0,1:T(8,128)S(1)}, s32[256,50]{0,1:T(8,128)}, u32[]{:S(2)}) copy-start(s32[256,50]{0,1:T(8,128)} %param.10) | copy-start | bytes 153604
  40.7 6.8 %copy-start.6 = (s32[256]{0:T(256)S(1)}, s32[256]{0:T(256)}, u32[]{:S(2)}) copy-start(s32[256]{0:T(256)} %param.11) | copy-start | bytes 3076
  40.7 7.1 %copy-start.4 = (f32[256,50,4]{0,2,1:T(4,128)S(1)}, f32[256,50,4]{0,2,1:T(4,128)}, u32[]{:S(2)}) copy-start(f32[256,50,4]{0,2,1:T(4,128)} %param.12) | copy-start | bytes 614404
  40.7 57.3 %all-to-all-start.1 = ((bf16[128,128,128]{2,1,0:T(8,128)(2,1)}), bf16[128,128,128]{2,1,0:T(8,128)(2,1)}, u32[]{:S(2)}, u32[]{:S(2)}) async-start(bf16[128,128,128]{2,1,0:T(8,128)(2,1)} %bitcast.24), calls=%async_computation.1 | async-start | bytes 8388608 | tf_op jit(solution)/shard_map/all_to_all | solution.py:406
  46.4 2.7 copy-start.2
  191.5 5.6 %copy-start.3 = (bf16[4,256,256]{2,1,0:T(8,128)(2,1)S(1)}, bf16[4,256,256]{2,1,0:T(8,128)(2,1)}, u32[]{:S(2)}) copy-start(bf16[4,256,256]{2,1,0:T(8,128)(2,1)} %get-tuple-element.4) | copy-start | bytes 1572868
  191.5 57.1 %all-to-all-start.2 = ((bf16[128,128,128]{2,1,0:T(8,128)(2,1)}), bf16[128,128,128]{2,1,0:T(8,128)(2,1)}, u32[]{:S(2)}, u32[]{:S(2)}) async-start(bf16[128,128,128]{2,1,0:T(8,128)(2,1)} %bitcast.26), calls=%async_computation.2 | async-start | bytes 8388608 | tf_op jit(solution)/shard_map/all_to_all | solution.py:406

commit v2 on v1

--- a/solution.py
+++ b/solution.py
@@ -11,6 +11,7 @@
 EPS = 1e-06
 LP = 64
 UG = 8
+BATCH = 5
 HALF = 128
 MIB = 1024 * 1024
 F32 = jnp.float32
@@ -26,7 +27,7 @@
 
 
 def two(i):
-    return pl.ds(pl.multiple_of(2 * i, 2), 2)
+    return pl.ds(pl.multiple_of(i, 2), 2)
 
 
 def split_rows(src, dst, rows, step=512):
@@ -43,15 +44,16 @@
 
 def fetch_kernel(slots, ids, table, out, wide, stage):
     rows = table.shape[0]
+    lists = ids.shape[0] // slots
     split_rows(table, wide, rows)
 
     def body(c, carry):
         for j in range(slots):
-            stage[pl.ds(2 * j, 2), :] = wide[two(ids[c * slots + j]), :]
+            stage[pl.ds(2 * j, 2), :] = wide[two(ids.at[pl.ds(j * lists, lists)][c]), :]
         out[pl.ds(pl.multiple_of(c * 2 * slots, 2 * slots), 2 * slots), :] = stage[...].astype(BF16)
         return carry
 
-    lax.fori_loop(0, ids.shape[0] // slots, body, 0)
+    lax.fori_loop(0, lists, body, 0)
 
 
 def fetch_rows(ids, table, slots):
@@ -64,43 +66,65 @@
         out_specs=vmem(),
         scratch_shapes=[pltpu.VMEM((2 * rows, HALF), F32), pltpu.VMEM((2 * slots, HALF), F32)],
         compiler_params=pltpu.CompilerParams(vmem_limit_bytes=40 * MIB),
-    )(ids, table)
-
-
-def return_kernel(slots, ids, grads, out, total, stage):
+    )(2 * ids.reshape(-1, slots).T.reshape(-1), table)
+
+
+def add_lines(totals, count, batch, line_of, value_of):
+    def load(n):
+        lines = [line_of(n * batch + j) for j in range(batch)]
+        return [(at, totals[n % 2][at, :]) for at in lines]
+
+    held = load(0)
+    for n in range(count // batch):
+        later = load(n + 1) if (n + 1) * batch < count else None
+        for j, (at, old) in enumerate(held):
+            totals[n % 2][at, :] = old + value_of(n * batch + j)
+        held = later
+
+
+def return_kernel(slots, feed, ids, grads, out, total0, total1, stage):
     step = pl.program_id(0)
-    feed = ids.shape[0] * 2 // grads.shape[0]
     chunk = grads.shape[0]
+    totals = (total0, total1)
+    lists = ids.shape[0] // slots
+    part = lists // feed
+    batch = 8
 
     @pl.when(step == 0)
     def _():
         def clear(c, carry):
-            total[pl.ds(pl.multiple_of(c * 512, 512), 512), :] = jnp.zeros((512, HALF), F32)
+            at = pl.ds(pl.multiple_of(c * 512, 512), 512)
+            for total in totals:
+                total[at, :] = jnp.zeros((512, HALF), F32)
             return carry
 
-        lax.fori_loop(0, (total.shape[0] - 16) // 512, clear, 0)
+        lax.fori_loop(0, (total0.shape[0] - 16) // 512, clear, 0)
 
     @pl.when(step < feed)
     def _():
         stage[...] = grads[...].astype(F32)
 
         def body(c, carry):
-            for b in range(2):
-                base = c * 64 + b * 32
-                at = [two(ids[step * (chunk // 2) + base + j]) for j in range(32)]
-                held = [total[at[j], :] for j in range(32)]
-                for j in range(32):
-                    total[at[j], :] = held[j] + stage[two(base + j), :]
+            given = stage.at[pl.ds(pl.multiple_of(c * 2 * slots, 2 * slots), 2 * slots), :]
+
+            add_lines(
+                totals,
+                slots,
+                batch,
+                lambda j: two(ids.at[pl.ds(j * lists, lists)][step * part + c]),
+                lambda j: given[pl.ds(2 * j, 2), :],
+            )
             return carry
 
-        lax.fori_loop(0, chunk // 128, body, 0)
+        lax.fori_loop(0, part, body, 0)
 
     @pl.when(step >= feed)
     def _():
         rows = out.shape[0]
         at = pl.multiple_of((step - feed) * 2 * rows, 2 * rows)
         for h in range(2):
-            out[:, h * HALF : (h + 1) * HALF] = total[pl.ds(at + h, rows, stride=2), :]
+            lines = pl.ds(at + h, rows, stride=2)
+            out[:, h * HALF : (h + 1) * HALF] = total0[lines, :] + total1[lines, :]
 
 
 def return_rows(ids, grads, rows, slots):
@@ -108,22 +132,22 @@
     drain = 8
     chunk = grads.shape[0] // feed
     return pl.pallas_call(
-        functools.partial(return_kernel, slots),
+        functools.partial(return_kernel, slots, feed),
         name="return_rows",
         grid=(feed + drain,),
         out_shape=jax.ShapeDtypeStruct((rows, 2 * HALF), F32),
         in_specs=[smem(), pl.BlockSpec((chunk, HALF), lambda i: (jnp.minimum(i, feed - 1), 0))],
         out_specs=pl.BlockSpec((rows // drain, 2 * HALF), lambda i: (jnp.maximum(i - feed, 0), 0)),
-        scratch_shapes=[pltpu.VMEM((2 * rows + 16, HALF), F32), pltpu.VMEM((chunk, HALF), F32)],
+        scratch_shapes=[pltpu.VMEM((2 * rows + 16, HALF), F32)] * 2 + [pltpu.VMEM((chunk, HALF), F32)],
         compiler_params=pltpu.CompilerParams(vmem_limit_bytes=40 * MIB),
-    )(ids, grads)
+    )(2 * ids.reshape(-1, slots).T.reshape(-1), grads)
 
 
 def route_kernel(
     interests, hist_len,
     slots, fetched, bilinear, first_logits, live, cotangent, same,
     capsules, slot_grads,
-    wide, rows, stage, logits, w0, w1, w2, z0, z1, pooled, q0, q1, g0, g1, g2, s0, s1, s2,
+    wide, more, rows, stage_a, stage_b, logits, w0, w1, w2, z0, z1, pooled, q0, q1, g0, g1, g2, s0, s1, s2,
     same_buf, same_sem,
 ):
     groups = live.shape[0]
@@ -176,7 +200,7 @@
     def loop(count, body):
         lax.fori_loop(0, count, lambda i, c: (body(i), c)[1], 0)
 
-    def over_groups(stages, unroll=2):
+    def over_groups(stages, unroll=8):
         def body(i):
             ids = [i * unroll + j for j in range(unroll)]
             held = [() for _ in ids]
@@ -220,16 +244,27 @@
         wide[at, :] = fetched[at, :].astype(F32)
 
     loop(fetched.shape[0] // split_dense, widen)
-    stage[...] = jnp.zeros_like(stage)
-
-    def first(g):
-        for u in range(UG):
-            for l in range(hist_len):
-                slot = slots[g * (UG * hist_len) + u * hist_len + l]
-                stage[pl.ds(2 * (u * LP + l), 2), :] = wide[two(slot), :]
+    for stage in (stage_a, stage_b):
+        stage[...] = jnp.zeros_like(stage)
+
+    def line_of(g, j):
+        return two(slots.at[pl.ds(j * groups, groups)][g])
+
+    def place(j):
+        return pl.ds(2 * (j // hist_len * LP + j % hist_len), 2)
+
+    behaviors = UG * hist_len
+
+    def gather(g, stage):
+        for j in range(behaviors):
+            stage[place(j), :] = wide[line_of(g, j), :]
+
+    def first(g, stage):
         at = pl.ds(pl.multiple_of(g * width, width), width)
-        for h in range(2):
-            rows[at, h * HALF : (h + 1) * HALF] = stage[pl.ds(h, width, stride=2), :].astype(BF16)
+        dense = jnp.concatenate(
+            [stage[pl.ds(h, width, stride=2), :].astype(BF16) for h in range(2)], axis=1
+        )
+        rows[at, :] = dense
         start = jnp.concatenate(
             [
                 jnp.broadcast_to(first_logits[pl.ds(g * interests + k, 1), :], (UG, width))
@@ -240,9 +275,17 @@
         lanes(logits, g)[...] = start
         weights = coupling(start, g)
         lanes(w0, g)[...] = weights
-        put_pooled(g, jnp.dot(weights.astype(BF16), block(g), preferred_element_type=F32))
-
-    loop(groups, first)
+        put_pooled(g, jnp.dot(weights.astype(BF16), dense, preferred_element_type=F32))
+
+    gather(0, stage_a)
+
+    def first_pair(i):
+        gather(2 * i + 1, stage_b)
+        first(2 * i, stage_a)
+        gather(jnp.minimum(2 * i + 2, groups - 1), stage_a)
+        first(2 * i + 1, stage_b)
+
+    loop(groups // 2, first_pair)
     forward(s0, q0)
 
     def turn(q, w, last):
@@ -298,23 +341,30 @@
     turn_back(g1, w1, z0, True)
     backward(s0, g0)
 
-    def copy_same(g):
-        slot = lax.rem(g, 2)
+    pairs = groups // 2
+
+    def copy_same(i):
+        slot = lax.rem(i, 2)
         return pltpu.make_async_copy(
-            same.at[pl.ds(pl.multiple_of(g * width, width), width), :],
+            same.at[pl.ds(pl.multiple_of((2 * i + 1) * width, width), 2 * width), :],
             same_buf.at[slot],
             same_sem.at[slot],
         )
 
+    head = pltpu.make_async_copy(
+        same.at[pl.ds(0, width), :], same_buf.at[1, pl.ds(0, width), :], same_sem.at[1]
+    )
+    head.start()
     copy_same(0).start()
 
     def clear(c):
         at = pl.ds(pl.multiple_of(c * split_dense, split_dense), split_dense)
-        wide[at, :] = jnp.zeros((split_dense, HALF), F32)
+        for total in (wide, more):
+            total[at, :] = jnp.zeros((split_dense, HALF), F32)
 
     loop(fetched.shape[0] // split_dense, clear)
 
-    def last(g):
+    def spread(g, equal, stage):
         coefs = jnp.concatenate(
             [lanes(w, g)[...].astype(BF16) for w in (w0, w1, w2)]
             + [lanes(z, g)[...] for z in (z0, z1)],
@@ -322,35 +372,46 @@
         )
         basis = jnp.concatenate([gathered(b, g) for b in (g0, g1, g2, q0, q1)], axis=0)
         grads = tn(coefs, basis).astype(BF16)
-
-        @pl.when(g + 1 < groups)
-        def _():
-            copy_same(g + 1).start()
-
-        copy_same(g).wait()
         part = width // 2
         for p in range(2):
             merged = jnp.dot(
-                same_buf[lax.rem(g, 2), p * part : (p + 1) * part, :],
+                equal[p * part : (p + 1) * part, :],
                 grads[p * part : (p + 1) * part],
                 preferred_element_type=F32,
             )
             for h in range(2):
                 stage[pl.ds(2 * p * part + h, part, stride=2), :] = merged[:, h * HALF : (h + 1) * HALF]
-        batch = hist_len // 2
-        for u in range(UG):
-            for b in range(2):
-                ls = range(b * batch, (b + 1) * batch)
-                at = [two(slots[g * (UG * hist_len) + u * hist_len + l]) for l in ls]
-                held = [wide[a, :] for a in at]
-                for a, value, l in zip(at, held, ls):
-                    wide[a, :] = value + stage[pl.ds(2 * (u * LP + l), 2), :]
-
-    loop(groups, last)
+
+    def scatter(g, stage):
+        add_lines(
+            (wide, more),
+            behaviors,
+            BATCH,
+            lambda j: line_of(g, j),
+            lambda j: stage[place(j), :],
+        )
+
+    head.wait()
+    spread(0, same_buf.at[1, pl.ds(0, width), :], stage_a)
+
+    def last_pair(i):
+        copy_same(i).wait()
+
+        @pl.when(i + 1 < pairs)
+        def _():
+            copy_same(i + 1).start()
+
+        equal = same_buf.at[lax.rem(i, 2)]
+        scatter(2 * i, stage_a)
+        spread(2 * i + 1, equal.at[pl.ds(0, width), :], stage_b)
+        scatter(2 * i + 1, stage_b)
+        spread(jnp.minimum(2 * i + 2, groups - 1), equal.at[pl.ds(width, width), :], stage_a)
+
+    loop(pairs, last_pair)
 
     def emit(c):
         at = pl.ds(pl.multiple_of(c * split_dense, split_dense), split_dense)
-        slot_grads[at, :] = wide[at, :].astype(BF16)
+        slot_grads[at, :] = (wide[at, :] + more[at, :]).astype(BF16)
 
     loop(fetched.shape[0] // split_dense, emit)
 
@@ -361,11 +422,11 @@
     groups = users_here // UG
     width = UG * LP
     pad = LP - hist_len
-    ids = jnp.pad(slots, ((0, 0), (0, pad)), constant_values=-1).reshape(users_here // 4, 4 * LP)
+    ids = jnp.pad(slots, ((0, UG), (0, pad)), constant_values=-1).reshape(-1, 4 * LP)
     place = jnp.arange(4 * LP, dtype=jnp.int32)
-    batch = place // LP * 2 + (place % LP >= hist_len // 2)
+    batch = place // LP * LP + place % LP // BATCH
     same = (ids[:, :, None] == ids[:, None, :]) & (batch[:, None] == batch[None, :])
-    same = same.astype(BF16).reshape(users_here * LP, 4 * LP)
+    same = same.astype(BF16).reshape(-1, 4 * LP)
     live = (jnp.arange(LP, dtype=jnp.int32)[None, :] < lengths[:, None]).astype(F32)
     live = live.reshape(groups, width)
     first_logits = jnp.pad(jnp.transpose(init_logits, (0, 2, 1)), ((0, 0), (0, 0), (0, pad)))
@@ -373,6 +434,7 @@
     first_logits = jnp.transpose(first_logits, (0, 2, 1, 3)).reshape(groups * interests, width)
     cotangent = jnp.transpose(interest_grad, (1, 0, 2))
     lines = groups * interests * UG
+    lines_of = (2 * slots).reshape(groups, UG * hist_len).T.reshape(-1)
     per_user = pltpu.VMEM((interests, users_here, feature), F32)
     capsules, slot_grads = pl.pallas_call(
         functools.partial(route_kernel, interests, hist_len),
@@ -385,15 +447,17 @@
         out_specs=(vmem(), vmem()),
         scratch_shapes=[
             pltpu.VMEM(fetched.shape, F32),
+            pltpu.VMEM(fetched.shape, F32),
             pltpu.VMEM((users_here * LP, feature), BF16),
+            pltpu.VMEM((2 * width, HALF), F32),
             pltpu.VMEM((2 * width, HALF), F32),
         ]
         + [pltpu.VMEM((lines, width), F32)] * 4
         + [pltpu.VMEM((lines, width), BF16)] * 2
         + [per_user] * 9
-        + [pltpu.VMEM((2, width, 4 * LP), BF16), pltpu.SemaphoreType.DMA((2,))],
+        + [pltpu.VMEM((2, 2 * width, 4 * LP), BF16), pltpu.SemaphoreType.DMA((2,))],
         compiler_params=pltpu.CompilerParams(vmem_limit_bytes=60 * MIB),
-    )(slots.reshape(-1), fetched, bilinear, first_logits, live, cotangent, same)
+    )(lines_of, fetched, bilinear, first_logits, live, cotangent, same)
     return jnp.transpose(capsules, (1, 0, 2)), slot_grads
 
 

time: 272 us -> 227 us (0.83)
  Pallas kernels: 129 us -> 84.6 us
  waiting for transfers between devices: 91.3 us -> 85.5 us
  other arithmetic: 7.46 us -> 12.3 us
    pallas_call x1, Pallas kernels: 93.5 us -> 61.4 us  [route(): pl.pallas_call(functools.partial(route_kernel, interests, hist_len), name...]
    pallas_call x1, Pallas kernels: 22.4 us -> 15.6 us  [return_rows(): pl.pallas_call(functools.partial(return_kernel, slots, feed), name='retur...]
    all_to_all x2, waiting for transfers between devices: 91.3 us -> 85.5 us  [exchange(): lax.all_to_all(value, ('gx', 'gy'), split_axis=0, concat_axis=0, tiled=True)]
    convert_element_type x1, other arithmetic: 5.9 us -> 11.5 us  [route(): same = same.astype(BF16).reshape(-1, 4 * LP)]
    pallas_call x1, Pallas kernels: 12.7 us -> 7.6 us  [fetch_rows(): pl.pallas_call(functools.partial(fetch_kernel, slots), name='fetch_rows',...]
  transfers between devices with their start and end apart: 2 -> 2, of which waited for: 2 -> 2; matrix products, arithmetic and copies ran while one was open for 4% -> 8% of each run, Pallas kernels for 0% -> 0%
where the time goes in v2:
time: 227 us; the launch traced here: 226 us
  waiting for transfers between devices  85.5 us (38%)
  Pallas kernels  84.6 us (37%)
  blocking collectives  20.9 us (9%)
  other arithmetic  12.3 us (5%)
  starting transfers between devices  11.2 us (5%)
  local copies, waits for them, and re-layouts  10.4 us (5%)
    all_to_all x2, waiting for transfers between devices, exchange(): lax.all_to_all(value, ('gx', 'gy'), split_axis=0, concat_axis=0, tiled=True)  85.5 us
    pallas_call x1, Pallas kernels, route(): pl.pallas_call(functools.partial(route_kernel, interests, hist_len), name...  61.4 us
    all_to_all x1, blocking collectives, exchange(): lax.all_to_all(value, ('gx', 'gy'), split_axis=0, concat_axis=0, tiled=True)  20.9 us
    pallas_call x1, Pallas kernels, return_rows(): pl.pallas_call(functools.partial(return_kernel, slots, feed), name='retur...  15.6 us
    convert_element_type x1, other arithmetic, route(): same = same.astype(BF16).reshape(-1, 4 * LP)  11.5 us
    all_to_all x2, starting transfers between devices, exchange(): lax.all_to_all(value, ('gx', 'gy'), split_axis=0, concat_axis=0, tiled=True)  11.2 us
    unnamed x19, local copies, waits for them, and re-layouts  7.8 us
    pallas_call x1, Pallas kernels, fetch_rows(): pl.pallas_call(functools.partial(fetch_kernel, slots), name='fetch_rows',...  7.6 us
  transfers between devices with their start and end apart: 2, of which 2 were waited for; matrix products, arithmetic and copies ran while one was open for 8% of the time, Pallas kernels for 0%

profile of v2, /device:TPU:1, one launch (start us, length us, event | category | flops | bytes accessed | tf_op | source)
XLA Modules:
  0.0 225.7 jit_solution(13082636021210328909)
XLA Ops:
  0.6 0.8 copy.31
  1.5 20.9 %all_to_all.34 = s32[128,1,64]{2,1,0:T(1,128)S(1)} all-to-all(s32[128,1,64]{2,1,0:T(1,128)S(1)} %bitcast.46), channel_id=1, replica_groups=mesh['gx'=8,'gy'=16] {'gx','gy'}, dimensions={0} | all-to-all | bytes 65536 | tf_op jit(solution)/shard_map/all_to_all | solution.py:470
  22.4 0.1 copy.32
  22.5 0.0 copy-start.1
  22.5 2.2 copy-done.1
  24.7 7.6 %fetch_rows.1 = bf16[16384,128]{1,0:T(8,128)(2,1)S(1)} custom-call(s32[8192]{0:T(1024)S(1)} %get-tuple-element.15.ids, bf16[8192,256]{1,0:T(8,128)(2,1)S(1)} %copy-done.1), custom_call_target="tpu_custom_call" | custom-call | tf_op jit(solution)/shard_map/fetch_rows/pallas_call | solution.py:61
  32.3 0.0 copy-start
  32.3 2.0 copy-done
  34.3 0.0 copy-start.4
  34.3 0.0 copy-start.6
  34.3 0.0 copy-start.5
  34.3 5.7 %all-to-all-start.1 = ((bf16[128,128,128]{2,1,0:T(8,128)(2,1)}), bf16[128,128,128]{2,1,0:T(8,128)(2,1)}, u32[]{:S(2)}, u32[]{:S(2)}) async-start(bf16[128,128,128]{2,1,0:T(8,128)(2,1)} %bitcast.40), calls=%async_computation.1 | async-start | bytes 8388608 | tf_op jit(solution)/shard_map/all_to_all | solution.py:470
  40.0 0.0 copy-done.4
  40.0 0.0 copy-start.2
  40.0 0.1 copy.39
  40.1 0.1 eq.39
  40.2 0.1 eq.41
  40.3 0.1 lt.29
  40.4 0.0 copy-done.6
  40.4 0.1 lt.31
  40.5 0.1 copy.29
  40.6 0.1 reshape.132
  40.7 0.1 lt.32
  40.8 0.1 lt.33
  40.9 0.1 copy.30
  41.0 0.7 reshape.133.slots
  41.7 0.0 copy-done.5
  41.7 0.2 copy.33
  42.0 0.1 copy.34
  42.1 0.9 reshape.135.first_logits
  42.9 0.0 copy-done.2
  42.9 1.2 copy.41
  44.2 0.1 broadcast_compare_fusion
  44.3 11.5 %fusion.1.same = bf16[16896,256]{1,0:T(8,128)(2,1)} fusion(s32[66,256]{1,0:T(8,128)S(1)} %eq.41, s32[16896]{0:T(1024)S(1)} %eq.39, pred[256,256]{1,0:T(8,128)(4,1)S(1)} %broadcast_compare_fusion), kind=kLoop, calls=%fused_computation.2 | loop fusion | flops 12976128 | bytes 8851456 | tf_op jit(solution)/shard_map/convert_element_type | solution.py:429
  55.8 0.6 compare_convert_fusion.live
  56.4 35.2 %all-to-all-done.1 = bf16[128,128,128]{2,1,0:T(8,128)(2,1)} async-done(((bf16[128,128,128]{2,1,0:T(8,128)(2,1)}), bf16[128,128,128]{2,1,0:T(8,128)(2,1)}, u32[]{:S(2)}, u32[]{:S(2)}) %all-to-all-start.1) | async-done | bytes 4194336 | tf_op jit(solution)/shard_map/all_to_all | solution.py:470
  91.6 61.4 %route_users.1 = (bf16[4,256,256]{2,1,0:T(8,128)(2,1)}, bf16[16384,128]{1,0:T(8,128)(2,1)}) custom-call(s32[12800]{0:T(1024)} %reshape.133.slots, bf16[16384,128]{1,0:T(8,128)(2,1)} %bitcast.6.fetched, bf16[256,1024]{1,0:T(8,128)(2,1)} %bilinear.1, f32[128,512]{1,0:T(8,128)} %reshape.135.first_logits, f32[32,512]{1,0:T(8,128)} %compare_convert_fusion.live, ...), custom_call_target="tpu_custom_call" | custom-call | tf_op jit(solution)/shard_map/route_users/pallas_call | solution.py:439
  153.0 0.0 copy-start.3
  153.1 5.6 %all-to-all-start.2 = ((bf16[128,128,128]{2,1,0:T(8,128)(2,1)}), bf16[128,128,128]{2,1,0:T(8,128)(2,1)}, u32[]{:S(2)}, u32[]{:S(2)}) async-start(bf16[128,128,128]{2,1,0:T(8,128)(2,1)} %bitcast.42), calls=%async_computation.2 | async-start | bytes 8388608 | tf_op jit(solution)/shard_map/all_to_all | solution.py:470
  158.7 0.0 copy-done.3
  158.7 1.2 copy.38
  159.9 50.3 %all-to-all-done.2 = bf16[128,128,128]{2,1,0:T(8,128)(2,1)} async-done(((bf16[128,128,128]{2,1,0:T(8,128)(2,1)}), bf16[128,128,128]{2,1,0:T(8,128)(2,1)}, u32[]{:S(2)}, u32[]{:S(2)}) %all-to-all-start.2) | async-done | bytes 4194336 | tf_op jit(solution)/shard_map/all_to_all | solution.py:470
  210.2 15.6 %return_rows.1 = f32[8192,256]{1,0:T(8,128)} custom-call(s32[8192]{0:T(1024)S(1)} %get-tuple-element.14.ids, bf16[16384,128]{1,0:T(8,128)(2,1)} %bitcast.17.grads), custom_call_target="tpu_custom_call" | custom-call | tf_op jit(solution)/shard_map/return_rows/pallas_call | solution.py:134
  (6 shorter events, 0.1 us)
Async XLA Ops:
  22.5 2.2 copy-start.1
  32.3 2.0 copy-start
  34.3 5.7 %copy-start.4 = (s32[256,50]{0,1:T(8,128)S(1)}, s32[256,50]{0,1:T(8,128)}, u32[]{:S(2)}) copy-start(s32[256,50]{0,1:T(8,128)} %param.10) | copy-start | bytes 153604
  34.3 6.1 %copy-start.6 = (s32[256]{0:T(256)S(1)}, s32[256]{0:T(256)}, u32[]{:S(2)}) copy-start(s32[256]{0:T(256)} %param.11) | copy-start | bytes 3076
  34.3 7.4 %copy-start.5 = (f32[256,50,4]{0,2,1:T(4,128)S(1)}, f32[256,50,4]{0,2,1:T(4,128)}, u32[]{:S(2)}) copy-start(f32[256,50,4]{0,2,1:T(4,128)} %param.12) | copy-start | bytes 614404
  34.3 57.3 %all-to-all-start.1 = ((bf16[128,128,128]{2,1,0:T(8,128)(2,1)}), bf16[128,128,128]{2,1,0:T(8,128)(2,1)}, u32[]{:S(2)}, u32[]{:S(2)}) async-start(bf16[128,128,128]{2,1,0:T(8,128)(2,1)} %bitcast.40), calls=%async_computation.1 | async-start | bytes 8388608 | tf_op jit(solution)/shard_map/all_to_all | solution.py:470
  40.0 3.0 %copy-start.2 = (f32[256,4,256]{2,1,0:T(4,128)S(1)}, f32[256,4,256]{2,1,0:T(4,128)}, u32[]{:S(2)}) copy-start(f32[256,4,256]{2,1,0:T(4,128)} %param.13) | copy-start | bytes 3145732
  153.0 5.6 %copy-start.3 = (bf16[4,256,256]{2,1,0:T(8,128)(2,1)S(1)}, bf16[4,256,256]{2,1,0:T(8,128)(2,1)}, u32[]{:S(2)}) copy-start(bf16[4,256,256]{2,1,0:T(8,128)(2,1)} %get-tuple-element.4) | copy-start | bytes 1572868
  153.1 57.1 %all-to-all-start.2 = ((bf16[128,128,128]{2,1,0:T(8,128)(2,1)}), bf16[128,128,128]{2,1,0:T(8,128)(2,1)}, u32[]{:S(2)}, u32[]{:S(2)}) async-start(bf16[128,128,128]{2,1,0:T(8,128)(2,1)} %bitcast.42), calls=%async_computation.2 | async-start | bytes 8388608 | tf_op jit(solution)/shard_map/all_to_all | solution.py:470

commit v3 on v2

--- a/solution.py
+++ b/solution.py
@@ -16,6 +16,7 @@
 MIB = 1024 * 1024
 F32 = jnp.float32
 BF16 = jnp.bfloat16
+MESH = pl.DeviceIdType.MESH
 
 
 def vmem():
@@ -30,43 +31,170 @@
     return pl.ds(pl.multiple_of(i, 2), 2)
 
 
-def split_rows(src, dst, rows, step=512):
-    def body(c, carry):
-        at = pl.multiple_of(c * step, step)
+def peer(step, sizes):
+    a, b, c, d = step % 4, step // 4 % 4, step // 16 % 4, step // 64
+    gx, gy = lax.axis_index("gx"), lax.axis_index("gy")
+    z = (gx // 2 + a + b) % 4
+    core = (gx + a // 2 + d) % 2
+    y = (gy // 4 + a + b + c) % 4
+    x = (gy + a) % 4
+    return z * 2 + core, y * 4 + x
+
+
+def greet(sizes):
+    barrier = pltpu.get_barrier_semaphore()
+
+    def body(step, carry):
+        pl.semaphore_signal(barrier, inc=1, device_id=peer(step, sizes), device_id_type=MESH)
+        return carry
+
+    lax.fori_loop(1, sizes[0] * sizes[1], body, 0)
+    return barrier
+
+
+def send(step, sizes, source, target, send_sem, recv_sem):
+    gx, gy = peer(step, sizes)
+    me = lax.axis_index("gx") * sizes[1] + lax.axis_index("gy")
+    pltpu.make_async_remote_copy(
+        src_ref=source.at[gx * sizes[1] + gy],
+        dst_ref=target.at[me],
+        send_sem=send_sem,
+        recv_sem=recv_sem,
+        device_id=(gx, gy),
+        device_id_type=MESH,
+    ).start()
+
+
+def all_but_one(ref, sem):
+    part = ref.at[pl.ds(0, ref.shape[0] - 1)]
+    pltpu.make_async_copy(part, part, sem).wait()
+
+
+def fetch_kernel(
+    sizes, slots, asked, table, fetched, wanted,
+    narrow, wide, stage, found, ids, table_sem, own_sem, ids_sem, sems,
+):
+    owners = sizes[0] * sizes[1]
+    rows = table.shape[0]
+    me = lax.axis_index("gx") * sizes[1] + lax.axis_index("gy")
+    fill = pltpu.make_async_copy(table, narrow, table_sem)
+    fill.start()
+    own = pltpu.make_async_copy(asked.at[me], wanted.at[me], own_sem)
+    own.start()
+    barrier = greet(sizes)
+    fill.wait()
+
+    def widen(c, carry):
+        at = pl.ds(pl.multiple_of(c * 512, 512), 512)
         for h in range(2):
-            dst[pl.ds(2 * at + h, step, stride=2), :] = src[
-                pl.ds(at, step), h * HALF : (h + 1) * HALF
-            ].astype(F32)
+            wide[at, h, :] = narrow[at, h * HALF : (h + 1) * HALF].astype(F32)
         return carry
 
-    lax.fori_loop(0, rows // step, body, 0)
-
-
-def fetch_kernel(slots, ids, table, out, wide, stage):
-    rows = table.shape[0]
-    lists = ids.shape[0] // slots
-    split_rows(table, wide, rows)
-
-    def body(c, carry):
+    early = rows // 512 * 5 // 8
+    lax.fori_loop(0, early, widen, 0)
+    pl.semaphore_wait(barrier, owners - 1)
+
+    def ask(step, carry):
+        send(step, sizes, asked, wanted, sems.at[0], sems.at[1])
+        return carry
+
+    lax.fori_loop(1, owners, ask, 0)
+    lax.fori_loop(early, rows // 512, widen, 0)
+    wide[rows] = jnp.zeros((2, HALF), F32)
+    own.wait()
+    all_but_one(asked, sems.at[0])
+    all_but_one(wanted, sems.at[1])
+    load = pltpu.make_async_copy(wanted, ids, ids_sem)
+    load.start()
+    load.wait()
+
+    def gather(block):
         for j in range(slots):
-            stage[pl.ds(2 * j, 2), :] = wide[two(ids.at[pl.ds(j * lists, lists)][c]), :]
-        out[pl.ds(pl.multiple_of(c * 2 * slots, 2 * slots), 2 * slots), :] = stage[...].astype(BF16)
+            stage[pl.ds(2 * j, 2), :] = wide[ids[block, 0, j]]
+        found[block] = stage[...].astype(BF16)
+
+    gather(me)
+    keep = pltpu.make_async_copy(found.at[me], fetched.at[me], own_sem)
+
+    def serve(step, carry):
+        gx, gy = peer(step, sizes)
+        gather(gx * sizes[1] + gy)
+
+        @pl.when(step > 1)
+        def _():
+            send(step - 1, sizes, found, fetched, sems.at[2], sems.at[3])
+
         return carry
 
-    lax.fori_loop(0, lists, body, 0)
-
-
-def fetch_rows(ids, table, slots):
-    rows = table.shape[0]
+    lax.fori_loop(1, owners, serve, 0)
+    keep.start()
+    send(owners - 1, sizes, found, fetched, sems.at[2], sems.at[3])
+    keep.wait()
+    all_but_one(found, sems.at[2])
+    all_but_one(fetched, sems.at[3])
+
+
+def fetch_rows(asked, table, sizes, slots):
+    rows, feature = table.shape
+    owners = asked.shape[0]
+    hbm = pl.BlockSpec(memory_space=pl.ANY)
     return pl.pallas_call(
-        functools.partial(fetch_kernel, slots),
+        functools.partial(fetch_kernel, sizes, slots),
         name="fetch_rows",
-        out_shape=jax.ShapeDtypeStruct((2 * ids.shape[0], HALF), BF16),
-        in_specs=[smem(), vmem()],
-        out_specs=vmem(),
-        scratch_shapes=[pltpu.VMEM((2 * rows, HALF), F32), pltpu.VMEM((2 * slots, HALF), F32)],
-        compiler_params=pltpu.CompilerParams(vmem_limit_bytes=40 * MIB),
-    )(2 * ids.reshape(-1, slots).T.reshape(-1), table)
+        out_shape=(
+            jax.ShapeDtypeStruct((owners, 2 * slots, HALF), BF16),
+            jax.ShapeDtypeStruct(asked.shape, jnp.int32),
+        ),
+        in_specs=[vmem(), hbm],
+        out_specs=(hbm, vmem()),
+        scratch_shapes=[
+            pltpu.VMEM((rows, feature), BF16),
+            pltpu.VMEM((rows + 4, 2, HALF), F32),
+            pltpu.VMEM((2 * slots, HALF), F32),
+            pltpu.VMEM((owners, 2 * slots, HALF), BF16),
+            pltpu.SMEM(asked.shape, jnp.int32),
+            pltpu.SemaphoreType.DMA,
+            pltpu.SemaphoreType.DMA,
+            pltpu.SemaphoreType.DMA,
+            pltpu.SemaphoreType.DMA((4,)),
+        ],
+        compiler_params=pltpu.CompilerParams(
+            collective_id=0, has_side_effects=True, vmem_limit_bytes=40 * MIB
+        ),
+    )(asked, table)
+
+
+def exchange_kernel(sizes, given, taken, own_sem, sems):
+    owners = sizes[0] * sizes[1]
+    me = lax.axis_index("gx") * sizes[1] + lax.axis_index("gy")
+    barrier = greet(sizes)
+    own = pltpu.make_async_copy(given.at[me], taken.at[me], own_sem)
+    own.start()
+    pl.semaphore_wait(barrier, owners - 1)
+
+    def serve(step, carry):
+        send(step, sizes, given, taken, sems.at[0], sems.at[1])
+        return carry
+
+    lax.fori_loop(1, owners, serve, 0)
+    own.wait()
+    all_but_one(given, sems.at[0])
+    all_but_one(taken, sems.at[1])
+
+
+def exchange(value, sizes):
+    hbm = pl.BlockSpec(memory_space=pl.ANY)
+    return pl.pallas_call(
+        functools.partial(exchange_kernel, sizes),
+        name="exchange",
+        out_shape=jax.ShapeDtypeStruct(value.shape, value.dtype),
+        in_specs=[hbm],
+        out_specs=hbm,
+        scratch_shapes=[pltpu.SemaphoreType.DMA, pltpu.SemaphoreType.DMA((2,))],
+        compiler_params=pltpu.CompilerParams(
+            collective_id=1, has_side_effects=True, vmem_limit_bytes=40 * MIB
+        ),
+    )(value)
 
 
 def add_lines(totals, count, batch, line_of, value_of):
@@ -140,15 +268,14 @@
         out_specs=pl.BlockSpec((rows // drain, 2 * HALF), lambda i: (jnp.maximum(i - feed, 0), 0)),
         scratch_shapes=[pltpu.VMEM((2 * rows + 16, HALF), F32)] * 2 + [pltpu.VMEM((chunk, HALF), F32)],
         compiler_params=pltpu.CompilerParams(vmem_limit_bytes=40 * MIB),
-    )(2 * ids.reshape(-1, slots).T.reshape(-1), grads)
+    )(ids.T.reshape(-1), grads)
 
 
 def route_kernel(
     interests, hist_len,
-    slots, fetched, bilinear, first_logits, live, cotangent, same,
+    slots, fetched, bilinear, first_logits, live, cotangent, keys,
     capsules, slot_grads,
     wide, more, rows, stage_a, stage_b, logits, w0, w1, w2, z0, z1, pooled, q0, q1, g0, g1, g2, s0, s1, s2,
-    same_buf, same_sem,
 ):
     groups = live.shape[0]
     width = UG * LP
@@ -341,22 +468,6 @@
     turn_back(g1, w1, z0, True)
     backward(s0, g0)
 
-    pairs = groups // 2
-
-    def copy_same(i):
-        slot = lax.rem(i, 2)
-        return pltpu.make_async_copy(
-            same.at[pl.ds(pl.multiple_of((2 * i + 1) * width, width), 2 * width), :],
-            same_buf.at[slot],
-            same_sem.at[slot],
-        )
-
-    head = pltpu.make_async_copy(
-        same.at[pl.ds(0, width), :], same_buf.at[1, pl.ds(0, width), :], same_sem.at[1]
-    )
-    head.start()
-    copy_same(0).start()
-
     def clear(c):
         at = pl.ds(pl.multiple_of(c * split_dense, split_dense), split_dense)
         for total in (wide, more):
@@ -364,7 +475,7 @@
 
     loop(fetched.shape[0] // split_dense, clear)
 
-    def spread(g, equal, stage):
+    def spread(g, stage):
         coefs = jnp.concatenate(
             [lanes(w, g)[...].astype(BF16) for w in (w0, w1, w2)]
             + [lanes(z, g)[...] for z in (z0, z1)],
@@ -374,8 +485,10 @@
         grads = tn(coefs, basis).astype(BF16)
         part = width // 2
         for p in range(2):
+            key = keys[pl.ds(2 * g + p, 1), :]
+            column = jnp.transpose(jnp.broadcast_to(key, (UG, part)))[:, :1]
             merged = jnp.dot(
-                equal[p * part : (p + 1) * part, :],
+                jnp.where(column == key, 1.0, 0.0).astype(BF16),
                 grads[p * part : (p + 1) * part],
                 preferred_element_type=F32,
             )
@@ -391,23 +504,15 @@
             lambda j: stage[place(j), :],
         )
 
-    head.wait()
-    spread(0, same_buf.at[1, pl.ds(0, width), :], stage_a)
+    spread(0, stage_a)
 
     def last_pair(i):
-        copy_same(i).wait()
-
-        @pl.when(i + 1 < pairs)
-        def _():
-            copy_same(i + 1).start()
-
-        equal = same_buf.at[lax.rem(i, 2)]
         scatter(2 * i, stage_a)
-        spread(2 * i + 1, equal.at[pl.ds(0, width), :], stage_b)
+        spread(2 * i + 1, stage_b)
         scatter(2 * i + 1, stage_b)
-        spread(jnp.minimum(2 * i + 2, groups - 1), equal.at[pl.ds(width, width), :], stage_a)
-
-    loop(pairs, last_pair)
+        spread(jnp.minimum(2 * i + 2, groups - 1), stage_a)
+
+    loop(groups // 2, last_pair)
 
     def emit(c):
         at = pl.ds(pl.multiple_of(c * split_dense, split_dense), split_dense)
@@ -422,11 +527,9 @@
     groups = users_here // UG
     width = UG * LP
     pad = LP - hist_len
-    ids = jnp.pad(slots, ((0, UG), (0, pad)), constant_values=-1).reshape(-1, 4 * LP)
-    place = jnp.arange(4 * LP, dtype=jnp.int32)
-    batch = place // LP * LP + place % LP // BATCH
-    same = (ids[:, :, None] == ids[:, None, :]) & (batch[:, None] == batch[None, :])
-    same = same.astype(BF16).reshape(-1, 4 * LP)
+    batch = jnp.arange(hist_len, dtype=jnp.int32) // BATCH + LP * (jnp.arange(users_here) % 4)[:, None]
+    keys = (slots * (4 * LP) + batch).astype(F32)
+    keys = jnp.pad(keys, ((0, 0), (0, pad)), constant_values=-1.0).reshape(-1, 4 * LP)
     live = (jnp.arange(LP, dtype=jnp.int32)[None, :] < lengths[:, None]).astype(F32)
     live = live.reshape(groups, width)
     first_logits = jnp.pad(jnp.transpose(init_logits, (0, 2, 1)), ((0, 0), (0, 0), (0, pad)))
@@ -443,7 +546,7 @@
             jax.ShapeDtypeStruct((interests, users_here, feature), BF16),
             jax.ShapeDtypeStruct(fetched.shape, BF16),
         ),
-        in_specs=[smem()] + [vmem()] * 5 + [pl.BlockSpec(memory_space=pl.ANY)],
+        in_specs=[smem()] + [vmem()] * 6,
         out_specs=(vmem(), vmem()),
         scratch_shapes=[
             pltpu.VMEM(fetched.shape, F32),
@@ -454,28 +557,23 @@
         ]
         + [pltpu.VMEM((lines, width), F32)] * 4
         + [pltpu.VMEM((lines, width), BF16)] * 2
-        + [per_user] * 9
-        + [pltpu.VMEM((2, 2 * width, 4 * LP), BF16), pltpu.SemaphoreType.DMA((2,))],
+        + [per_user] * 9,
         compiler_params=pltpu.CompilerParams(vmem_limit_bytes=60 * MIB),
-    )(lines_of, fetched, bilinear, first_logits, live, cotangent, same)
+    )(lines_of, fetched, bilinear, first_logits, live, cotangent, keys)
     return jnp.transpose(capsules, (1, 0, 2)), slot_grads
 
 
-def local(item_table, bilinear, requests, history, lengths, init_logits, interest_grad):
+def local(sizes, item_table, bilinear, requests, history, lengths, init_logits, interest_grad):
     asked = requests[0]
     owners, slots = asked.shape
     table_rows = item_table.shape[0]
-
-    def exchange(value):
-        return lax.all_to_all(value, ("gx", "gy"), split_axis=0, concat_axis=0, tiled=True)
-
-    wanted = exchange(asked).reshape(-1)
-    found = fetch_rows(jnp.maximum(wanted, 0), item_table, slots)
-    fetched = exchange(found)
+    asked = jnp.where(asked >= 0, asked, table_rows)
+    asked = jnp.pad(asked, ((0, 0), (0, 128 - slots)))[:, None, :]
+    fetched, wanted = fetch_rows(asked, item_table, sizes, slots)
+    fetched = fetched.reshape(-1, HALF)
     capsules, slot_grads = route(history, fetched, bilinear, lengths, init_logits, interest_grad)
-    returned = exchange(slot_grads)
-    targets = jnp.where(wanted >= 0, wanted, table_rows)
-    return capsules, return_rows(targets, returned, table_rows, slots)
+    returned = exchange(slot_grads.reshape(owners, 2 * slots, HALF), sizes).reshape(-1, HALF)
+    return capsules, return_rows(2 * wanted[:, 0, :slots], returned, table_rows, slots)
 
 
 def solution(mesh):
@@ -490,7 +588,7 @@
         P(both, None, None),
     )
     return jax.shard_map(
-        local,
+        functools.partial(local, (mesh.shape["gx"], mesh.shape["gy"])),
         mesh=mesh,
         in_specs=placed,
         out_specs=(P(both, None, None), P(both, None)),

time: 227 us -> 231 us (1.018)
  Pallas kernels: 84.6 us -> 208 us
  waiting for transfers between devices: 85.5 us -> 0 us
  blocking collectives: 20.9 us -> 0 us
  starting transfers between devices: 11.2 us -> 0 us
  other arithmetic: 12.3 us -> 1.62 us
  local copies, waits for them, and re-layouts: 10.4 us -> 20 us
    pallas_call x1 -> x2, Pallas kernels: 7.6 us -> 135 us  [the longest x1 76.2 us: fetch_rows(): pl.pallas_call(functools.partial(fetch_kernel, sizes, slots), name='fetch...]
    all_to_all x2 -> x0, waiting for transfers between devices: 85.5 us -> none  [exchange(): lax.all_to_all(value, ('gx', 'gy'), split_axis=0, concat_axis=0, tiled=True)]
    all_to_all x1 -> x0, blocking collectives: 20.9 us -> none  [exchange(): lax.all_to_all(value, ('gx', 'gy'), split_axis=0, concat_axis=0, tiled=True)]
    all_to_all x2 -> x0, starting transfers between devices: 11.2 us -> none  [exchange(): lax.all_to_all(value, ('gx', 'gy'), split_axis=0, concat_axis=0, tiled=True)]
    convert_element_type x1, other arithmetic: 11.5 us -> 0.9 us  [route(): keys = (slots * (4 * LP) + batch).astype(F32)]
    unnamed x19 -> x17, local copies, waits for them, and re-layouts: 7.8 us -> 16.1 us
    pallas_call x1, Pallas kernels: 61.4 us -> 57.8 us  [route(): pl.pallas_call(functools.partial(route_kernel, interests, hist_len), name...]
  transfers between devices with their start and end apart: 2 -> 0, of which waited for: 2 -> 0; matrix products, arithmetic and copies ran while one was open for 8% -> 0% of each run, Pallas kernels for 0% -> 0%
where the time goes in v3:
time: 231 us
  Pallas kernels  208 us (90%)
  local copies, waits for them, and re-layouts  20 us (9%)
    pallas_call x1, Pallas kernels, fetch_rows(): pl.pallas_call(functools.partial(fetch_kernel, sizes, slots), name='fetch...  76.2 us
    pallas_call x1, Pallas kernels, exchange(): pl.pallas_call(functools.partial(exchange_kernel, sizes), name='exchange'...  58.9 us
    pallas_call x1, Pallas kernels, route(): pl.pallas_call(functools.partial(route_kernel, interests, hist_len), name...  57.8 us
    unnamed x17, local copies, waits for them, and re-layouts  16.1 us
    pallas_call x1, Pallas kernels, return_rows(): pl.pallas_call(functools.partial(return_kernel, slots, feed), name='retur...  15.5 us

profile of v3, /device:TPU:1, one launch (start us, length us, event | category | flops | bytes accessed | tf_op | source)
XLA Modules:
  0.0 230.7 jit_solution(17016088140870374208)
XLA Ops:
  0.6 0.0 copy-start.5
  0.7 0.1 lt.29
  0.8 0.8 lt.31
  1.6 0.9 copy.16
  2.5 0.9 add_convert_fusion
  3.4 0.1 copy.23
  3.5 0.7 reshape.68.keys
  4.2 0.1 lt.32
  4.3 0.1 lt.33
  4.4 0.6 compare_convert_fusion.live
  5.0 0.1 copy.14
  5.2 0.1 reshape.63
  5.3 0.1 copy.15
  5.4 0.7 reshape.64.slots
  6.1 1.1 copy.17
  7.3 0.1 copy.18
  7.4 0.9 reshape.67.first_logits
  8.2 0.0 copy-done.5
  8.2 1.2 copy.25
  9.4 0.0 copy-start.2
  9.4 2.2 copy-done.2
  11.6 76.2 %fetch_rows.1 = (bf16[128,128,128]{2,1,0:T(8,128)(2,1)S(1)}, s32[128,1,128]{2,1,0:T(1,128)S(1)}) custom-call(s32[128,1,128]{2,1,0:T(1,128)S(1)} %bitcast.25, bf16[8192,256]{1,0:T(8,128)(2,1)S(1)} %copy-done.2), custom_call_target="tpu_custom_call" | custom-call | tf_op jit(solution)/shard_map/fetch_rows/pallas_call | solution.py:141
  87.8 0.0 copy-start.3
  87.8 2.0 copy-done.3
  89.8 57.8 %route_users.1 = (bf16[4,256,256]{2,1,0:T(8,128)(2,1)}, bf16[16384,128]{1,0:T(8,128)(2,1)}) custom-call(s32[12800]{0:T(1024)} %reshape.64.slots, bf16[16384,128]{1,0:T(8,128)(2,1)} %bitcast.23, bf16[256,1024]{1,0:T(8,128)(2,1)} %bilinear.1, f32[128,512]{1,0:T(8,128)} %reshape.67.first_logits, f32[32,512]{1,0:T(8,128)} %compare_convert_fusion.live, ...), custom_call_target="tpu_custom_call" | custom-call | tf_op jit(solution)/shard_map/route_users/pallas_call | solution.py:542
  147.6 2.2 copy.22
  149.8 0.0 copy-start.4
  149.8 2.2 copy-done.4
  152.0 58.9 %exchange.1 = bf16[128,128,128]{2,1,0:T(8,128)(2,1)S(1)} custom-call(bf16[128,128,128]{2,1,0:T(8,128)(2,1)S(1)} %bitcast.24), custom_call_target="tpu_custom_call" | custom-call | tf_op jit(solution)/shard_map/exchange/pallas_call | solution.py:187
  210.9 0.0 copy-start
  210.9 2.0 copy-done
  212.9 0.1 slice_multiply_fusion
  212.9 0.1 copy.21
  213.0 0.0 copy-start.1
  213.0 2.2 copy-done.1
  215.2 15.5 %return_rows.1 = f32[8192,256]{1,0:T(8,128)} custom-call(s32[8192]{0:T(1024)S(1)} %bitcast.26, bf16[16384,128]{1,0:T(8,128)(2,1)S(1)} %bitcast.22), custom_call_target="tpu_custom_call" | custom-call | tf_op jit(solution)/shard_map/return_rows/pallas_call | solution.py:262
  (7 shorter events, 0.1 us)
Async XLA Ops:
  0.6 7.6 %copy-start.5 = (f32[256,4,256]{2,1,0:T(4,128)S(1)}, f32[256,4,256]{2,1,0:T(4,128)}, u32[]{:S(2)}) copy-start(f32[256,4,256]{2,1,0:T(4,128)} %param.13) | copy-start | bytes 3145732
  9.4 2.2 copy-start.2
  87.8 2.0 copy-start.3
  149.8 2.2 copy-start.4
  210.9 2.0 copy-start
  213.0 2.2 copy-start.1

commit v4 on v3

--- a/solution.py
+++ b/solution.py
@@ -31,7 +31,7 @@
     return pl.ds(pl.multiple_of(i, 2), 2)
 
 
-def peer(step, sizes):
+def peer(step):
     a, b, c, d = step % 4, step // 4 % 4, step // 16 % 4, step // 64
     gx, gy = lax.axis_index("gx"), lax.axis_index("gy")
     z = (gx // 2 + a + b) % 4
@@ -41,19 +41,28 @@
     return z * 2 + core, y * 4 + x
 
 
-def greet(sizes):
+def partners():
+    gx, gy = lax.axis_index("gx"), lax.axis_index("gy")
+    z = [(gx // 2 + i) % 4 * 2 for i in range(4)]
+    core = [(gx + i) % 2 for i in range(2)]
+    y = [(gy // 4 + i) % 4 * 4 for i in range(4)]
+    x = [(gy + i) % 4 for i in range(4)]
+    found = []
+    for step in range(1, 128):
+        a, b, c, d = step % 4, step // 4 % 4, step // 16 % 4, step // 64
+        found.append((z[(a + b) % 4] + core[(a // 2 + d) % 2], y[(a + b + c) % 4] + x[a]))
+    return found
+
+
+def greet(others):
     barrier = pltpu.get_barrier_semaphore()
-
-    def body(step, carry):
-        pl.semaphore_signal(barrier, inc=1, device_id=peer(step, sizes), device_id_type=MESH)
-        return carry
-
-    lax.fori_loop(1, sizes[0] * sizes[1], body, 0)
+    for other in others:
+        pl.semaphore_signal(barrier, inc=1, device_id=other, device_id_type=MESH)
     return barrier
 
 
-def send(step, sizes, source, target, send_sem, recv_sem):
-    gx, gy = peer(step, sizes)
+def send(other, sizes, source, target, send_sem, recv_sem):
+    gx, gy = other
     me = lax.axis_index("gx") * sizes[1] + lax.axis_index("gy")
     pltpu.make_async_remote_copy(
         src_ref=source.at[gx * sizes[1] + gy],
@@ -81,7 +90,8 @@
     fill.start()
     own = pltpu.make_async_copy(asked.at[me], wanted.at[me], own_sem)
     own.start()
-    barrier = greet(sizes)
+    others = partners()
+    barrier = greet(others)
     fill.wait()
 
     def widen(c, carry):
@@ -94,11 +104,8 @@
     lax.fori_loop(0, early, widen, 0)
     pl.semaphore_wait(barrier, owners - 1)
 
-    def ask(step, carry):
-        send(step, sizes, asked, wanted, sems.at[0], sems.at[1])
-        return carry
-
-    lax.fori_loop(1, owners, ask, 0)
+    for other in others:
+        send(other, sizes, asked, wanted, sems.at[0], sems.at[1])
     lax.fori_loop(early, rows // 512, widen, 0)
     wide[rows] = jnp.zeros((2, HALF), F32)
     own.wait()
@@ -117,18 +124,18 @@
     keep = pltpu.make_async_copy(found.at[me], fetched.at[me], own_sem)
 
     def serve(step, carry):
-        gx, gy = peer(step, sizes)
+        gx, gy = peer(step)
         gather(gx * sizes[1] + gy)
 
         @pl.when(step > 1)
         def _():
-            send(step - 1, sizes, found, fetched, sems.at[2], sems.at[3])
+            send(peer(step - 1), sizes, found, fetched, sems.at[2], sems.at[3])
 
         return carry
 
     lax.fori_loop(1, owners, serve, 0)
     keep.start()
-    send(owners - 1, sizes, found, fetched, sems.at[2], sems.at[3])
+    send(peer(owners - 1), sizes, found, fetched, sems.at[2], sems.at[3])
     keep.wait()
     all_but_one(found, sems.at[2])
     all_but_one(fetched, sems.at[3])
@@ -137,7 +144,7 @@
 def fetch_rows(asked, table, sizes, slots):
     rows, feature = table.shape
     owners = asked.shape[0]
-    hbm = pl.BlockSpec(memory_space=pl.ANY)
+    hbm = pl.BlockSpec(memory_space=pltpu.HBM)
     return pl.pallas_call(
         functools.partial(fetch_kernel, sizes, slots),
         name="fetch_rows",
@@ -167,23 +174,21 @@
 def exchange_kernel(sizes, given, taken, own_sem, sems):
     owners = sizes[0] * sizes[1]
     me = lax.axis_index("gx") * sizes[1] + lax.axis_index("gy")
-    barrier = greet(sizes)
+    others = partners()
+    barrier = greet(others)
     own = pltpu.make_async_copy(given.at[me], taken.at[me], own_sem)
     own.start()
     pl.semaphore_wait(barrier, owners - 1)
 
-    def serve(step, carry):
-        send(step, sizes, given, taken, sems.at[0], sems.at[1])
-        return carry
-
-    lax.fori_loop(1, owners, serve, 0)
+    for other in others:
+        send(other, sizes, given, taken, sems.at[0], sems.at[1])
     own.wait()
     all_but_one(given, sems.at[0])
     all_but_one(taken, sems.at[1])
 
 
 def exchange(value, sizes):
-    hbm = pl.BlockSpec(memory_space=pl.ANY)
+    hbm = pl.BlockSpec(memory_space=pltpu.HBM)
     return pl.pallas_call(
         functools.partial(exchange_kernel, sizes),
         name="exchange",
@@ -275,7 +280,7 @@
     interests, hist_len,
     slots, fetched, bilinear, first_logits, live, cotangent, keys,
     capsules, slot_grads,
-    wide, more, rows, stage_a, stage_b, logits, w0, w1, w2, z0, z1, pooled, q0, q1, g0, g1, g2, s0, s1, s2,
+    narrow, narrow_sems, wide, more, rows, stage_a, stage_b, logits, w0, w1, w2, z0, z1, pooled, q0, q1, g0, g1, g2, s0, s1, final,
 ):
     groups = live.shape[0]
     width = UG * LP
@@ -365,12 +370,27 @@
             out[k] = nt(grad.astype(BF16), mapping(k))
 
     split_dense = 1024
+    parts = narrow_sems.shape[0]
+    share = fetched.shape[0] // parts
+
+    def share_of(c):
+        return pl.ds(pl.multiple_of(c * share, share), share)
+
+    def copy_in(c):
+        return pltpu.make_async_copy(fetched.at[share_of(c), :], narrow.at[share_of(c), :], narrow_sems.at[c])
+
+    def copy_out(c):
+        return pltpu.make_async_copy(narrow.at[share_of(c), :], slot_grads.at[share_of(c), :], narrow_sems.at[c])
+
+    loop(parts, lambda c: copy_in(c).start())
 
     def widen(c):
-        at = pl.ds(pl.multiple_of(c * split_dense, split_dense), split_dense)
-        wide[at, :] = fetched[at, :].astype(F32)
-
-    loop(fetched.shape[0] // split_dense, widen)
+        copy_in(c).wait()
+        for p in range(share // split_dense):
+            at = pl.ds(pl.multiple_of(c * share + p * split_dense, split_dense), split_dense)
+            wide[at, :] = narrow[at, :].astype(F32)
+
+    loop(parts, widen)
     for stage in (stage_a, stage_b):
         stage[...] = jnp.zeros_like(stage)
 
@@ -440,8 +460,11 @@
     for k in range(interests):
         summed = jnp.dot(pooled[k].astype(BF16), mapping(k), preferred_element_type=F32)
         grad, factor = squash_grad(summed, cotangent[k])
-        capsules[k] = (summed * factor).astype(BF16)
+        final[:, k, :] = summed * factor
         g2[k] = nt(grad.astype(BF16), mapping(k))
+
+    for u in range(0, final.shape[0], 64):
+        capsules[u : u + 64] = final[u : u + 64].astype(BF16)
 
     def turn_back(gr, w, z, add):
         def dots(g):
@@ -515,10 +538,13 @@
     loop(groups // 2, last_pair)
 
     def emit(c):
-        at = pl.ds(pl.multiple_of(c * split_dense, split_dense), split_dense)
-        slot_grads[at, :] = (wide[at, :] + more[at, :]).astype(BF16)
-
-    loop(fetched.shape[0] // split_dense, emit)
+        for p in range(share // split_dense):
+            at = pl.ds(pl.multiple_of(c * share + p * split_dense, split_dense), split_dense)
+            narrow[at, :] = (wide[at, :] + more[at, :]).astype(BF16)
+        copy_out(c).start()
+
+    loop(parts, emit)
+    loop(parts, lambda c: copy_out(c).wait())
 
 
 def route(slots, fetched, bilinear, lengths, init_logits, interest_grad):
@@ -539,16 +565,19 @@
     lines = groups * interests * UG
     lines_of = (2 * slots).reshape(groups, UG * hist_len).T.reshape(-1)
     per_user = pltpu.VMEM((interests, users_here, feature), F32)
+    hbm = pl.BlockSpec(memory_space=pltpu.HBM)
     capsules, slot_grads = pl.pallas_call(
         functools.partial(route_kernel, interests, hist_len),
         name="route_users",
         out_shape=(
-            jax.ShapeDtypeStruct((interests, users_here, feature), BF16),
+            jax.ShapeDtypeStruct((users_here, interests, feature), BF16),
             jax.ShapeDtypeStruct(fetched.shape, BF16),
         ),
-        in_specs=[smem()] + [vmem()] * 6,
-        out_specs=(vmem(), vmem()),
+        in_specs=[smem(), hbm] + [vmem()] * 5,
+        out_specs=(vmem(), hbm),
         scratch_shapes=[
+            pltpu.VMEM(fetched.shape, BF16),
+            pltpu.SemaphoreType.DMA((8,)),
             pltpu.VMEM(fetched.shape, F32),
             pltpu.VMEM(fetched.shape, F32),
             pltpu.VMEM((users_here * LP, feature), BF16),
@@ -557,10 +586,11 @@
         ]
         + [pltpu.VMEM((lines, width), F32)] * 4
         + [pltpu.VMEM((lines, width), BF16)] * 2
-        + [per_user] * 9,
+        + [per_user] * 8
+        + [pltpu.VMEM((users_here, interests, feature), F32)],
         compiler_params=pltpu.CompilerParams(vmem_limit_bytes=60 * MIB),
     )(lines_of, fetched, bilinear, first_logits, live, cotangent, keys)
-    return jnp.transpose(capsules, (1, 0, 2)), slot_grads
+    return capsules, slot_grads
 
 
 def local(sizes, item_table, bilinear, requests, history, lengths, init_logits, interest_grad):

time: 231 us -> 217 us (0.939)
  Pallas kernels: 208 us -> 196 us
    pallas_call x1, Pallas kernels: 76.2 us -> 68.5 us  [fetch_rows(): pl.pallas_call(functools.partial(fetch_kernel, sizes, slots), name='fetch...]
    pallas_call x1, Pallas kernels: 58.9 us -> 53.5 us  [exchange(): pl.pallas_call(functools.partial(exchange_kernel, sizes), name='exchange'...]
    unnamed x17 -> x16, local copies, waits for them, and re-layouts: 16.1 us -> 13.9 us
where the time goes in v4:
time: 217 us; the launch traced here: 216 us
  Pallas kernels  196 us (90%)
  local copies, waits for them, and re-layouts  17.8 us (8%)
    pallas_call x1, Pallas kernels, fetch_rows(): pl.pallas_call(functools.partial(fetch_kernel, sizes, slots), name='fetch...  68.5 us
    pallas_call x1, Pallas kernels, route(): pl.pallas_call(functools.partial(route_kernel, interests, hist_len), name...  58.7 us
    pallas_call x1, Pallas kernels, exchange(): pl.pallas_call(functools.partial(exchange_kernel, sizes), name='exchange'...  53.5 us
    pallas_call x1, Pallas kernels, return_rows(): pl.pallas_call(functools.partial(return_kernel, slots, feed), name='retur...  15.5 us
    unnamed x16, local copies, waits for them, and re-layouts  13.9 us

profile of v4, /device:TPU:1, one launch (start us, length us, event | category | flops | bytes accessed | tf_op | source)
XLA Modules:
  0.0 216.4 jit_solution(17092898629572131976)
XLA Ops:
  0.6 0.0 copy-start.5
  0.7 0.1 lt.29
  0.8 0.8 lt.31
  1.6 0.9 copy.15
  2.5 0.9 add_convert_fusion
  3.4 0.1 copy.21
  3.5 0.7 reshape.68.keys
  4.2 0.1 lt.32
  4.3 0.1 lt.33
  4.4 0.6 compare_convert_fusion.live
  5.0 0.1 copy.13
  5.1 0.1 reshape.63
  5.2 0.1 copy.14
  5.4 0.7 reshape.64.slots
  6.1 1.1 copy.16
  7.3 0.1 copy.17
  7.4 0.9 reshape.67.first_logits
  8.3 0.0 copy-done.5
  8.3 1.2 copy.23
  9.4 0.0 copy-start.2
  9.4 2.2 %copy-done.2 = bf16[8192,256]{1,0:T(8,128)(2,1)S(1)} copy-done((bf16[8192,256]{1,0:T(8,128)(2,1)S(1)}, bf16[8192,256]{1,0:T(8,128)(2,1)}, u32[]{:S(2)}) %copy-start.2) | copy-done | bytes 4194328
  11.6 68.5 %fetch_rows.1 = (bf16[128,128,128]{2,1,0:T(8,128)(2,1)S(1)}, s32[128,1,128]{2,1,0:T(1,128)S(1)}) custom-call(s32[128,1,128]{2,1,0:T(1,128)S(1)} %bitcast.24, bf16[8192,256]{1,0:T(8,128)(2,1)S(1)} %copy-done.2), custom_call_target="tpu_custom_call" | custom-call | tf_op jit(solution)/shard_map/fetch_rows/pallas_call | solution.py:148
  80.1 0.0 copy-start.3
  80.1 2.0 copy-done.3
  82.1 58.7 %route_users.1 = (bf16[256,4,256]{2,1,0:T(4,128)(2,1)}, bf16[16384,128]{1,0:T(8,128)(2,1)}) custom-call(s32[12800]{0:T(1024)} %reshape.64.slots, bf16[16384,128]{1,0:T(8,128)(2,1)} %bitcast.22, bf16[256,1024]{1,0:T(8,128)(2,1)} %bilinear.1, f32[128,512]{1,0:T(8,128)} %reshape.67.first_logits, f32[32,512]{1,0:T(8,128)} %compare_convert_fusion.live, ...), custom_call_target="tpu_custom_call" | custom-call | tf_op jit(solution)/shard_map/route_users/pallas_call | solution.py:569
  140.8 0.0 copy-start.4
  140.8 2.2 %copy-done.4 = bf16[16384,128]{1,0:T(8,128)(2,1)S(1)} copy-done((bf16[16384,128]{1,0:T(8,128)(2,1)S(1)}, bf16[16384,128]{1,0:T(8,128)(2,1)}, u32[]{:S(2)}) %copy-start.4) | copy-done | bytes 4194328
  143.0 53.5 %exchange.1 = bf16[128,128,128]{2,1,0:T(8,128)(2,1)S(1)} custom-call(bf16[128,128,128]{2,1,0:T(8,128)(2,1)S(1)} %bitcast.23), custom_call_target="tpu_custom_call" | custom-call | tf_op jit(solution)/shard_map/exchange/pallas_call | solution.py:192
  196.6 0.0 copy-start
  196.6 2.0 copy-done
  198.6 0.1 slice_multiply_fusion
  198.6 0.1 copy.20
  198.7 0.0 copy-start.1
  198.7 2.2 %copy-done.1 = bf16[128,128,128]{2,1,0:T(8,128)(2,1)S(1)} copy-done((bf16[128,128,128]{2,1,0:T(8,128)(2,1)S(1)}, bf16[128,128,128]{2,1,0:T(8,128)(2,1)}, u32[]{:S(2)}) %copy-start.1) | copy-done | bytes 4194328
  200.9 15.5 %return_rows.1 = f32[8192,256]{1,0:T(8,128)} custom-call(s32[8192]{0:T(1024)S(1)} %bitcast.25, bf16[16384,128]{1,0:T(8,128)(2,1)S(1)} %bitcast.21), custom_call_target="tpu_custom_call" | custom-call | tf_op jit(solution)/shard_map/return_rows/pallas_call | solution.py:267
  (7 shorter events, 0.1 us)
Async XLA Ops:
  0.6 7.7 %copy-start.5 = (f32[256,4,256]{2,1,0:T(4,128)S(1)}, f32[256,4,256]{2,1,0:T(4,128)}, u32[]{:S(2)}) copy-start(f32[256,4,256]{2,1,0:T(4,128)} %param.13) | copy-start | bytes 3145732
  9.4 2.2 %copy-start.2 = (bf16[8192,256]{1,0:T(8,128)(2,1)S(1)}, bf16[8192,256]{1,0:T(8,128)(2,1)}, u32[]{:S(2)}) copy-start(bf16[8192,256]{1,0:T(8,128)(2,1)} %table.1) | copy-start | bytes 12582916
  80.1 2.0 copy-start.3
  140.8 2.2 %copy-start.4 = (bf16[16384,128]{1,0:T(8,128)(2,1)S(1)}, bf16[16384,128]{1,0:T(8,128)(2,1)}, u32[]{:S(2)}) copy-start(bf16[16384,128]{1,0:T(8,128)(2,1)} %get-tuple-element.9) | copy-start | bytes 12582916
  196.6 2.0 copy-start
  198.7 2.2 %copy-start.1 = (bf16[128,128,128]{2,1,0:T(8,128)(2,1)S(1)}, bf16[128,128,128]{2,1,0:T(8,128)(2,1)}, u32[]{:S(2)}) copy-start(bf16[128,128,128]{2,1,0:T(8,128)(2,1)} %copy-done) | copy-start | bytes 12582916

commit v5 on v4

--- a/solution.py
+++ b/solution.py
@@ -166,7 +166,7 @@
             pltpu.SemaphoreType.DMA((4,)),
         ],
         compiler_params=pltpu.CompilerParams(
-            collective_id=0, has_side_effects=True, vmem_limit_bytes=40 * MIB
+            collective_id=0, has_side_effects=True, vmem_limit_bytes=61 * MIB
         ),
     )(asked, table)
 
@@ -197,7 +197,7 @@
         out_specs=hbm,
         scratch_shapes=[pltpu.SemaphoreType.DMA, pltpu.SemaphoreType.DMA((2,))],
         compiler_params=pltpu.CompilerParams(
-            collective_id=1, has_side_effects=True, vmem_limit_bytes=40 * MIB
+            collective_id=1, has_side_effects=True, vmem_limit_bytes=61 * MIB
         ),
     )(value)
 
@@ -272,7 +272,7 @@
         in_specs=[smem(), pl.BlockSpec((chunk, HALF), lambda i: (jnp.minimum(i, feed - 1), 0))],
         out_specs=pl.BlockSpec((rows // drain, 2 * HALF), lambda i: (jnp.maximum(i - feed, 0), 0)),
         scratch_shapes=[pltpu.VMEM((2 * rows + 16, HALF), F32)] * 2 + [pltpu.VMEM((chunk, HALF), F32)],
-        compiler_params=pltpu.CompilerParams(vmem_limit_bytes=40 * MIB),
+        compiler_params=pltpu.CompilerParams(vmem_limit_bytes=61 * MIB),
     )(ids.T.reshape(-1), grads)
 
 
@@ -553,7 +553,8 @@
     groups = users_here // UG
     width = UG * LP
     pad = LP - hist_len
-    batch = jnp.arange(hist_len, dtype=jnp.int32) // BATCH + LP * (jnp.arange(users_here) % 4)[:, None]
+    batch = jnp.arange(hist_len, dtype=jnp.int32) + hist_len * (jnp.arange(users_here) % 4)[:, None]
+    batch = batch // BATCH
     keys = (slots * (4 * LP) + batch).astype(F32)
     keys = jnp.pad(keys, ((0, 0), (0, pad)), constant_values=-1.0).reshape(-1, 4 * LP)
     live = (jnp.arange(LP, dtype=jnp.int32)[None, :] < lengths[:, None]).astype(F32)
@@ -588,7 +589,7 @@
         + [pltpu.VMEM((lines, width), BF16)] * 2
         + [per_user] * 8
         + [pltpu.VMEM((users_here, interests, feature), F32)],
-        compiler_params=pltpu.CompilerParams(vmem_limit_bytes=60 * MIB),
+        compiler_params=pltpu.CompilerParams(vmem_limit_bytes=61 * MIB),
     )(lines_of, fetched, bilinear, first_logits, live, cotangent, keys)
     return capsules, slot_grads
 

time: 217 us -> 211 us (0.972)
  local copies, waits for them, and re-layouts: 17.8 us -> 8.45 us
  Pallas kernels: 196 us -> 199 us
    unnamed x16 -> x8, local copies, waits for them, and re-layouts: 13.9 us -> 3.29 us
where the time goes in v5:
time: 211 us; the launch traced here: 210 us
  Pallas kernels  199 us (94%)
  local copies, waits for them, and re-layouts  8.45 us (4%)
    pallas_call x1, Pallas kernels, fetch_rows(): pl.pallas_call(functools.partial(fetch_kernel, sizes, slots), name='fetch...  69.6 us
    pallas_call x1, Pallas kernels, route(): pl.pallas_call(functools.partial(route_kernel, interests, hist_len), name...  58.7 us
    pallas_call x1, Pallas kernels, exchange(): pl.pallas_call(functools.partial(exchange_kernel, sizes), name='exchange'...  54.9 us
    pallas_call x1, Pallas kernels, return_rows(): pl.pallas_call(functools.partial(return_kernel, slots, feed), name='retur...  15.8 us

profile of v5, /device:TPU:1, one launch (start us, length us, event | category | flops | bytes accessed | tf_op | source)
XLA Modules:
  0.0 209.9 jit_solution(17448038307283626417)
XLA Ops:
  0.6 0.0 copy-start
  0.7 0.1 lt.29
  0.7 0.8 lt.31
  1.6 0.9 copy.15
  2.4 0.6 pad.12
  3.1 0.9 fusion.1
  4.0 0.1 copy.21
  4.1 0.7 reshape.55.keys
  4.8 0.1 lt.32
  4.9 0.1 lt.33
  5.0 0.6 compare_convert_fusion.live
  5.6 0.1 copy.13
  5.7 0.1 reshape.50
  5.8 0.1 copy.14
  6.0 0.7 reshape.51.slots
  6.7 1.1 copy.16
  7.9 0.1 copy.17
  8.0 0.9 reshape.54.first_logits
  8.8 0.0 copy-done
  8.8 1.2 copy.23
  10.0 69.6 %fetch_rows.1 = (bf16[128,128,128]{2,1,0:T(8,128)(2,1)}, s32[128,1,128]{2,1,0:T(1,128)}) custom-call(s32[128,1,128]{2,1,0:T(1,128)} %bitcast.26, bf16[8192,256]{1,0:T(8,128)(2,1)} %table.1), custom_call_target="tpu_custom_call" | custom-call | tf_op jit(solution)/shard_map/fetch_rows/pallas_call | solution.py:148
  79.6 58.7 %route_users.1 = (bf16[256,4,256]{2,1,0:T(4,128)(2,1)}, bf16[16384,128]{1,0:T(8,128)(2,1)}) custom-call(s32[12800]{0:T(1024)} %reshape.51.slots, bf16[16384,128]{1,0:T(8,128)(2,1)} %bitcast.22, bf16[256,1024]{1,0:T(8,128)(2,1)} %bilinear.1, f32[128,512]{1,0:T(8,128)} %reshape.54.first_logits, f32[32,512]{1,0:T(8,128)} %compare_convert_fusion.live, ...), custom_call_target="tpu_custom_call" | custom-call | tf_op jit(solution)/shard_map/route_users/pallas_call | solution.py:570
  138.4 0.0 copy-start.1
  138.4 54.9 %exchange.1 = bf16[128,128,128]{2,1,0:T(8,128)(2,1)} custom-call(bf16[128,128,128]{2,1,0:T(8,128)(2,1)} %bitcast.23), custom_call_target="tpu_custom_call" | custom-call | tf_op jit(solution)/shard_map/exchange/pallas_call | solution.py:192
  193.3 0.0 copy-done.1
  193.3 0.1 slice_multiply_fusion
  193.4 0.7 copy.20
  194.1 15.8 %return_rows.1 = f32[8192,256]{1,0:T(8,128)} custom-call(s32[8192]{0:T(1024)} %bitcast.29, bf16[16384,128]{1,0:T(8,128)(2,1)} %bitcast.21), custom_call_target="tpu_custom_call" | custom-call | tf_op jit(solution)/shard_map/return_rows/pallas_call | solution.py:267
  (5 shorter events, 0.1 us)
Async XLA Ops:
  0.6 8.2 %copy-start = (f32[256,4,256]{2,1,0:T(4,128)S(1)}, f32[256,4,256]{2,1,0:T(4,128)}, u32[]{:S(2)}) copy-start(f32[256,4,256]{2,1,0:T(4,128)} %param.13) | copy-start | bytes 3145732
  138.4 54.9 %copy-start.1 = (s32[128,1,128]{2,1,0:T(1,128)S(1)}, s32[128,1,128]{2,1,0:T(1,128)}, u32[]{:S(2)}) copy-start(s32[128,1,128]{2,1,0:T(1,128)} %get-tuple-element.8) | copy-start | bytes 196612

commit v6 on v5

--- a/solution.py
+++ b/solution.py
@@ -107,7 +107,6 @@
     for other in others:
         send(other, sizes, asked, wanted, sems.at[0], sems.at[1])
     lax.fori_loop(early, rows // 512, widen, 0)
-    wide[rows] = jnp.zeros((2, HALF), F32)
     own.wait()
     all_but_one(asked, sems.at[0])
     all_but_one(wanted, sems.at[1])
@@ -117,7 +116,7 @@
 
     def gather(block):
         for j in range(slots):
-            stage[pl.ds(2 * j, 2), :] = wide[ids[block, 0, j]]
+            stage[pl.ds(2 * j, 2), :] = wide[jnp.maximum(ids[block, 0, j], 0)]
         found[block] = stage[...].astype(BF16)
 
     gather(me)
@@ -156,7 +155,7 @@
         out_specs=(hbm, vmem()),
         scratch_shapes=[
             pltpu.VMEM((rows, feature), BF16),
-            pltpu.VMEM((rows + 4, 2, HALF), F32),
+            pltpu.VMEM((rows, 2, HALF), F32),
             pltpu.VMEM((2 * slots, HALF), F32),
             pltpu.VMEM((owners, 2 * slots, HALF), BF16),
             pltpu.SMEM(asked.shape, jnp.int32),
@@ -332,7 +331,7 @@
     def loop(count, body):
         lax.fori_loop(0, count, lambda i, c: (body(i), c)[1], 0)
 
-    def over_groups(stages, unroll=8):
+    def over_groups(stages, unroll=16):
         def body(i):
             ids = [i * unroll + j for j in range(unroll)]
             held = [() for _ in ids]
@@ -598,13 +597,12 @@
     asked = requests[0]
     owners, slots = asked.shape
     table_rows = item_table.shape[0]
-    asked = jnp.where(asked >= 0, asked, table_rows)
-    asked = jnp.pad(asked, ((0, 0), (0, 128 - slots)))[:, None, :]
-    fetched, wanted = fetch_rows(asked, item_table, sizes, slots)
+    fetched, wanted = fetch_rows(asked[:, None, :], item_table, sizes, slots)
+    wanted = jnp.where(wanted >= 0, 2 * wanted, 2 * table_rows)
     fetched = fetched.reshape(-1, HALF)
     capsules, slot_grads = route(history, fetched, bilinear, lengths, init_logits, interest_grad)
     returned = exchange(slot_grads.reshape(owners, 2 * slots, HALF), sizes).reshape(-1, HALF)
-    return capsules, return_rows(2 * wanted[:, 0, :slots], returned, table_rows, slots)
+    return capsules, return_rows(wanted[:, 0, :], returned, table_rows, slots)
 
 
 def solution(mesh):

time: 211 us -> 210 us (level)
  no operation moved by 1% of the time
where the time goes in v6:
time: 210 us; the launch traced here: 209 us
  Pallas kernels  198 us (94%)
  local copies, waits for them, and re-layouts  8.45 us (4%)
    pallas_call x1, Pallas kernels, fetch_rows(): pl.pallas_call(functools.partial(fetch_kernel, sizes, slots), name='fetch...  69.7 us
    pallas_call x1, Pallas kernels, route(): pl.pallas_call(functools.partial(route_kernel, interests, hist_len), name...  58 us
    pallas_call x1, Pallas kernels, exchange(): pl.pallas_call(functools.partial(exchange_kernel, sizes), name='exchange'...  54.7 us
    pallas_call x1, Pallas kernels, return_rows(): pl.pallas_call(functools.partial(return_kernel, slots, feed), name='retur...  15.8 us

profile of v6, /device:TPU:1, one launch (start us, length us, event | category | flops | bytes accessed | tf_op | source)
XLA Modules:
  0.0 209.0 jit_solution(6764417572675636315)
XLA Ops:
  0.6 0.0 copy-start
  0.7 0.1 lt.29
  0.7 0.8 lt.31
  1.6 1.5 copy.15
  3.1 0.9 fusion.1
  3.9 0.1 copy.21
  4.1 0.7 reshape.53.keys
  4.8 0.1 lt.32
  4.9 0.1 lt.33
  5.0 0.6 compare_convert_fusion.live
  5.6 0.1 copy.13
  5.7 0.1 reshape.48
  5.8 0.1 copy.14
  5.9 0.7 reshape.49.slots
  6.7 1.1 copy.16
  7.9 0.1 copy.17
  7.9 0.9 reshape.52.first_logits
  8.8 0.0 copy-done
  8.8 1.2 copy.23
  10.0 69.7 %fetch_rows.1 = (bf16[128,128,128]{2,1,0:T(8,128)(2,1)}, s32[128,1,64]{2,1,0:T(1,128)}) custom-call(s32[128,1,64]{2,1,0:T(1,128)} %bitcast.24, bf16[8192,256]{1,0:T(8,128)(2,1)} %table.1), custom_call_target="tpu_custom_call" | custom-call | tf_op jit(solution)/shard_map/fetch_rows/pallas_call | solution.py:147
  79.7 58.0 %route_users.1 = (bf16[256,4,256]{2,1,0:T(4,128)(2,1)}, bf16[16384,128]{1,0:T(8,128)(2,1)}) custom-call(s32[12800]{0:T(1024)} %reshape.49.slots, bf16[16384,128]{1,0:T(8,128)(2,1)} %bitcast.20, bf16[256,1024]{1,0:T(8,128)(2,1)} %bilinear.1, f32[128,512]{1,0:T(8,128)} %reshape.52.first_logits, f32[32,512]{1,0:T(8,128)} %compare_convert_fusion.live, ...), custom_call_target="tpu_custom_call" | custom-call | tf_op jit(solution)/shard_map/route_users/pallas_call | solution.py:569
  137.7 0.0 copy-start.1
  137.7 54.7 %exchange.1 = bf16[128,128,128]{2,1,0:T(8,128)(2,1)} custom-call(bf16[128,128,128]{2,1,0:T(8,128)(2,1)} %bitcast.21), custom_call_target="tpu_custom_call" | custom-call | tf_op jit(solution)/shard_map/exchange/pallas_call | solution.py:191
  192.4 0.0 copy-done.1
  192.4 0.1 compare_select_fusion
  192.5 0.7 copy.20
  193.2 15.8 %return_rows.1 = f32[8192,256]{1,0:T(8,128)} custom-call(s32[8192]{0:T(1024)} %bitcast.27, bf16[16384,128]{1,0:T(8,128)(2,1)} %bitcast.19), custom_call_target="tpu_custom_call" | custom-call | tf_op jit(solution)/shard_map/return_rows/pallas_call | solution.py:266
  (4 shorter events, 0.1 us)
Async XLA Ops:
  0.6 8.2 %copy-start = (f32[256,4,256]{2,1,0:T(4,128)S(1)}, f32[256,4,256]{2,1,0:T(4,128)}, u32[]{:S(2)}) copy-start(f32[256,4,256]{2,1,0:T(4,128)} %param.13) | copy-start | bytes 3145732
  137.7 54.7 %copy-start.1 = (s32[128,1,64]{2,1,0:T(1,128)S(1)}, s32[128,1,64]{2,1,0:T(1,128)}, u32[]{:S(2)}) copy-start(s32[128,1,64]{2,1,0:T(1,128)} %get-tuple-element.8) | copy-start | bytes 98308
